TPU v7x, 512 devices: a whole 4x4x16 slice. The times are simulated.
512 devices in a mesh: ctx: 128 (over y_hi, z, x), tp: 4 (over y_lo, core).
Axes of the slice: x: 4, y: 4 (y_hi: 2, y_lo: 2; y = y_hi * 2 + y_lo), z: 16, core: 2. Of those that a mesh axis runs over, the one named last changes fastest.
Arguments:
- residual: bfloat16 [32768, 8192], P('ctx', 'tp'), may hold values from -16 to 16
- features: bfloat16 [32768, 3, 8192], P('ctx', None, 'tp'), may hold values from -6 to 6
- short_taps: float32 [3, 3, 8192], P(None, None, 'tp'), may hold values from -3.5 to 3.5
- filter_taps: bfloat16 [512, 128], P('tp'), may hold values from -0.5 to 0.5
- skip_gain: float32 [8192], P('tp'), may hold values from -1 to 1
- norm_gain: float32 [8192], P('tp'), may hold values from 0.5 to 1.5
Outputs:
- normed: bfloat16 [32768, 8192], P('ctx', 'tp')
All inputs are finite; a program needn't handle non-finite values.
Results may differ from a plain program's by a relative error of at most 0.0065.
Values may be sent and summed in bfloat16 or wider, within the bound.
No kernel may reach another device: no remote copies, remote signals or barrier semaphores. Data moves between devices by JAX's collectives and lax.ppermute only.
A program may use at most 128 MiB of HBM per device.

v0:
```python
import jax
import jax.numpy as jnp
from jax import lax
from jax.sharding import PartitionSpec as P

D = 8192


def passed_along(block, axis, distance):
    devices = range(lax.axis_size(axis))
    route = [(i - distance, i) for i in devices if i - distance in devices]
    return lax.ppermute(block, axis, route)


def featurize(padded, weights):
    return (weights[0] * padded[2:] + weights[1] * padded[1:-1] + weights[2] * padded[:-2]).astype(
        jnp.bfloat16
    )


def toeplitz(taps, filter_len):
    groups = taps.shape[0]
    period = 3 * filter_len
    pattern = jnp.concatenate(
        [
            jnp.zeros((groups, 1), taps.dtype),
            jnp.flip(taps, 1),
            jnp.zeros((groups, 2 * filter_len - 1), taps.dtype),
        ],
        1,
    )
    tiled = jnp.tile(pattern, (1, filter_len))[:, : filter_len * (period - 1)]
    return tiled.reshape(groups, filter_len, period - 1)[:, :, : 2 * filter_len]


def on_device(residual, features, short_taps, filter_taps, skip_gain, norm_gain):
    tok_rows, _, channels = features.shape
    groups = filter_taps.shape[0]
    group_size = channels // groups
    filter_len = filter_taps.shape[1]
    blocks = tok_rows // filter_len
    front_rim = passed_along(features[tok_rows - 2 :], "ctx", 1)
    padded = jnp.concatenate([front_rim, features], 0)
    featured = featurize(padded, short_taps)
    gated_in = (featured[:, 1].astype(jnp.float32) * featured[:, 2].astype(jnp.float32)).astype(
        jnp.bfloat16
    )
    band_full = toeplitz(filter_taps, filter_len)
    lower_band = band_full[:, :, filter_len:]
    upper_band = band_full[:, :, :filter_len]
    stacked = gated_in.reshape(blocks, filter_len, groups, group_size)
    local_part = jnp.einsum(
        "gij,bjgs->bigs", lower_band, stacked, preferred_element_type=jnp.float32
    )
    carried = jnp.einsum("gij,bjgs->bigs", upper_band, stacked, preferred_element_type=jnp.float32)
    incoming = passed_along(
        carried[blocks - 1, : filter_len - 1].astype(jnp.bfloat16), "ctx", 1
    ).astype(jnp.float32)
    head_block = jnp.concatenate([incoming, jnp.zeros((1, groups, group_size), jnp.float32)], 0)
    carry_part = jnp.concatenate([head_block[None], carried[:-1]], 0)
    filtered = (local_part + carry_part).reshape(tok_rows, channels) + skip_gain * gated_in.astype(
        jnp.float32
    )
    stream = (residual.astype(jnp.float32) + featured[:, 0].astype(jnp.float32) * filtered).astype(
        jnp.bfloat16
    )
    stream_f = stream.astype(jnp.float32)
    sum_squares = lax.psum(jnp.sum(stream_f * stream_f, axis=1, keepdims=True), "tp")
    return (stream_f * lax.rsqrt(sum_squares / D + 1e-06) * norm_gain).astype(jnp.bfloat16)


def solution(mesh):
    in_specs = (
        P("ctx", "tp"),
        P("ctx", None, "tp"),
        P(None, None, "tp"),
        P("tp", None),
        P("tp"),
        P("tp"),
    )
    out_specs = P("ctx", "tp")
    return jax.shard_map(
        on_device, mesh=mesh, in_specs=in_specs, out_specs=out_specs, check_vma=False
    )
```

profile of v0, /device:TPU:25, one launch (start us, length us, event | category | flops | bytes accessed | tf_op | source)
XLA Modules:
  0.0 129.7 jit_solution(14201362467935955648)
XLA Ops:
  0.0 0.9 slice.48
  0.9 3.1 %collective-permute-start = (bf16[2,3,2048]{2,0,1:T(2,128)(2,1)S(1)}, bf16[2,3,2048]{2,0,1:T(2,128)(2,1)S(1)}, u32[]{:S(2)}, u32[]{:S(2)}) collective-permute-start(bf16[2,3,2048]{2,0,1:T(2,128)(2,1)S(1)} %slice.48), channel_id=1, source_target_pairs={{0,4},{4,8},{8,12},{12,16},{16,20},{20,24},{24,28},{28,32},{32,36}... | collective-permute-start | bytes 73736 | tf_op jit(solution)/shard_map/ppermute | solution.py:12
  4.1 0.8 rev.4
  4.9 0.1 pad.6.clone
  5.0 0.8 slice_bitcast_fusion.11
  5.8 0.1 maximum_maximum_fusion
  5.9 4.7 %copy.20 = bf16[256,3,2048]{0,2,1:T(8,128)(2,1)} copy(bf16[256,3,2048]{2,0,1:T(8,128)(2,1)} %param.7) | data formatting | bytes 6291456 | tf_op args[1]
  10.6 5.6 %tile.4 = bf16[128,128,384]{2,1,0:T(8,128)(2,1)} broadcast(bf16[128,384]{1,0:T(8,128)(2,1)S(1)} %maximum_maximum_fusion), dimensions={0,2} | broadcast | bytes 12681216 | tf_op jit(solution)/shard_map/tile | solution.py:32
  16.2 12.5 %copy.30 = bf16[16,8,128,384]{3,1,2,0:T(8,128)(2,1)S(1)} copy(bf16[16,8,128,384]{3,2,1,0:T(8,128)(2,1)} %bitcast.62) | data formatting | bytes 25165824
  28.7 5.1 %slice.65 = bf16[128,49024]{1,0:T(8,128)(2,1)} slice(bf16[128,49152]{1,0:T(8,128)(2,1)S(1)} %bitcast.63), slice={[0:128], [0:49024]} | slice | bytes 25100288 | tf_op jit(solution)/shard_map/slice | solution.py:32
  33.8 30.9 %reshape.28 = bf16[128,128,383]{2,1,0:T(8,128)(2,1)} reshape(bf16[128,49024]{1,0:T(8,128)(2,1)} %slice.65) | data formatting | bytes 25100288 | tf_op jit(solution)/shard_map/reshape | solution.py:33
  64.7 0.0 collective-permute-done
  64.7 1.6 %copy.21 = bf16[2,3,2048]{0,2,1:T(8,128)(2,1)} copy(bf16[2,3,2048]{2,0,1:T(2,128)(2,1)S(1)} %collective-permute-done) | data formatting | bytes 49152 | tf_op jit(solution)/shard_map/ppermute | solution.py:12
  66.2 10.5 %add_convert_fusion = bf16[256,3,2048]{0,2,1:T(8,128)(2,1)S(1)} fusion(bf16[256,3,2048]{0,2,1:T(8,128)(2,1)} %copy.20, bf16[2,3,2048]{0,2,1:T(8,128)(2,1)} %copy.21, f32[3,2048]{1,0:T(4,128)S(1)} %get-tuple-element.8, f32[3,2048]{1,0:T(4,128)S(1)} %get-tuple-element.9, f32[3,2048]{1,0:T(4,128)S(1)} %get-tuple-element.7), kind=kLoop, calls=%fused_computation | loop fusion | flops 23592960 | bytes 6389760 | tf_op jit(solution)/shard_map/convert_element_type | solution.py:16
  76.7 1.2 multiply_convert_fusion
  77.9 2.2 %convert_element_type.71 = bf16[2,128,128,16]{1,0,3,2:T(2,128)(2,1)} reshape(bf16[256,1,2048]{0,2,1:T(8,128)(2,1)} %multiply_convert_fusion) | data formatting | bytes 2097152 | tf_op jit(solution)/shard_map/convert_element_type | solution.py:45
  80.1 4.8 %fusion.9 = f32[2,128,128,16]{1,3,0,2:T(8,128)S(1)} fusion(bf16[128,128,383]{2,1,0:T(8,128)(2,1)} %reshape.28, bf16[2,128,128,16]{1,0,3,2:T(2,128)(2,1)} %convert_element_type.71), kind=kOutput, calls=%fused_computation.21 | convolution fusion | flops 134217728 | bytes 7340032 | tf_op jit(solution)/shard_map/gij,bjgs->bigs/dot_general | solution.py:55
  84.9 0.0 copy-start.1
  84.9 1.4 %copy-done.1 = f32[2,128,128,16]{1,3,0,2:T(8,128)} copy-done((f32[2,128,128,16]{1,3,0,2:T(8,128)}, f32[2,128,128,16]{1,3,0,2:T(8,128)S(1)}, u32[]{:S(2)}) %copy-start.1) | copy-done | bytes 2097176
  86.2 0.9 fusion.12
  87.1 3.1 %collective-permute-start.1 = (bf16[127,128,16]{0,2,1:T(8,128)(2,1)}, bf16[127,128,16]{0,2,1:T(8,128)(2,1)}, u32[]{:S(2)}, u32[]{:S(2)}) collective-permute-start(bf16[127,128,16]{0,2,1:T(8,128)(2,1)} %fusion.12), channel_id=1, source_target_pairs={{0,4},{4,8},{8,12},{12,16},{16,20},{20,24},{24,28},{28,32},{32,36}... | collective-permute-start | bytes 1560584 | tf_op jit(solution)/shard_map/ppermute | solution.py:12
  90.3 2.3 %copy.19 = bf16[256,2048]{0,1:T(8,128)(2,1)} copy(bf16[256,2048]{1,0:T(8,128)(2,1)} %param.6) | data formatting | bytes 2097152 | tf_op args[0]
  92.5 0.0 copy-start
  92.5 0.0 slice-start
  92.5 19.4 %collective-permute-done.1 = bf16[127,128,16]{0,2,1:T(8,128)(2,1)} collective-permute-done((bf16[127,128,16]{0,2,1:T(8,128)(2,1)}, bf16[127,128,16]{0,2,1:T(8,128)(2,1)}, u32[]{:S(2)}, u32[]{:S(2)}) %collective-permute-start.1) | collective-permute-done | bytes 520224 | tf_op jit(solution)/shard_map/ppermute | solution.py:12
  111.9 1.1 bitcast_convert_fusion
  113.0 0.0 copy-done
  113.0 0.0 slice-done
  113.0 4.5 %maximum_add_fusion = f32[2,128,128,16]{1,3,0,2:T(8,128)S(1)} fusion(f32[1,128,128,16]{1,3,0,2:T(8,128)S(1)} %slice-done, f32[1,128,128,16]{1,3,0,2:T(8,128)S(1)} %bitcast_convert_fusion, bf16[128,128,383]{2,1,0:T(8,128)(2,1)} %reshape.28, bf16[2,128,128,16]{1,0,3,2:T(2,128)(2,1)S(1)} %copy-done), kind=kOutput, calls=%fused_computation.18 | convolution fusion | flops 135266304 | bytes 9437184 | tf_op jit(solution)/shard_map/gij,bjgs->bigs/dot_general | solution.py:52
  117.6 0.0 copy-start.2
  117.6 0.0 copy-start.3
  117.6 1.1 copy.26
  118.7 0.1 copy-done.2
  118.8 0.0 copy-done.3
  118.8 0.0 copy-start.4
  118.8 1.7 %fusion.3 = (f32[256]{0:T(256)S(1)}, bf16[256,2048]{0,1:T(8,128)(2,1)}) fusion(f32[2048]{0:T(1024)S(1)} %copy-done.3, f32[256,8,2,128]{3,2,1,0:T(2,128)S(1)} %bitcast.64, bf16[256,3,2048]{0,2,1:T(8,128)(2,1)S(1)} %add_convert_fusion, bf16[256,2048]{0,1:T(8,128)(2,1)S(1)} %copy-done.2), kind=kLoop, calls=%fused_computation.11 | loop fusion | flops 7864064 | bytes 7349248 | tf_op jit(solution)/shard_map/reduce_sum | solution.py:68
  120.5 6.2 %psum.7 = f32[256,1]{0,1:T(1,128)S(1)} all-reduce(f32[256,1]{0,1:T(1,128)S(1)} %bitcast.65), channel_id=1, replica_groups=mesh['ctx'=128,'tp'=4] {'tp'}, use_global_device_ids=true, to_apply=%region_1.2 | all-reduce | flops 256 | bytes 2048 | tf_op jit(solution)/shard_map/psum | solution.py:68
  126.7 0.0 copy-done.4
  126.7 1.6 %fusion.5 = bf16[256,2048]{0,1:T(8,128)(2,1)S(1)} fusion(bf16[256,2048]{0,1:T(8,128)(2,1)} %get-tuple-element.6, f32[2048]{0:T(1024)S(1)} %copy-done.4, f32[256]{0:T(256)S(1)} %bitcast.66), kind=kLoop, calls=%fused_computation.13 | loop fusion | flops 2097152 | bytes 2106368 | tf_op jit(solution)/shard_map/convert_element_type | solution.py:69
  128.3 1.4 %copy.27 = bf16[256,2048]{1,0:T(8,128)(2,1)} copy(bf16[256,2048]{0,1:T(8,128)(2,1)S(1)} %fusion.5) | data formatting | bytes 2097152 | tf_op jit(solution)/shard_map/convert_element_type | solution.py:69
  (3 shorter events, 0.0 us)
Async XLA Ops:
  0.9 63.7 %collective-permute-start = (bf16[2,3,2048]{2,0,1:T(2,128)(2,1)S(1)}, bf16[2,3,2048]{2,0,1:T(2,128)(2,1)S(1)}, u32[]{:S(2)}, u32[]{:S(2)}) collective-permute-start(bf16[2,3,2048]{2,0,1:T(2,128)(2,1)S(1)} %slice.48), channel_id=1, source_target_pairs={{0,4},{4,8},{8,12},{12,16},{16,20},{20,24},{24,28},{28,32},{32,36}... | collective-permute-start | bytes 73736 | tf_op jit(solution)/shard_map/ppermute | solution.py:12
  84.9 1.4 %copy-start.1 = (f32[2,128,128,16]{1,3,0,2:T(8,128)}, f32[2,128,128,16]{1,3,0,2:T(8,128)S(1)}, u32[]{:S(2)}) copy-start(f32[2,128,128,16]{1,3,0,2:T(8,128)S(1)} %fusion.9) | copy-start | bytes 6291460
  87.1 24.7 %collective-permute-start.1 = (bf16[127,128,16]{0,2,1:T(8,128)(2,1)}, bf16[127,128,16]{0,2,1:T(8,128)(2,1)}, u32[]{:S(2)}, u32[]{:S(2)}) collective-permute-start(bf16[127,128,16]{0,2,1:T(8,128)(2,1)} %fusion.12), channel_id=1, source_target_pairs={{0,4},{4,8},{8,12},{12,16},{16,20},{20,24},{24,28},{28,32},{32,36}... | collective-permute-start | bytes 1560584 | tf_op jit(solution)/shard_map/ppermute | solution.py:12
  92.5 20.5 %copy-start = (bf16[2,128,128,16]{1,0,3,2:T(2,128)(2,1)S(1)}, bf16[2,128,128,16]{1,0,3,2:T(2,128)(2,1)}, u32[]{:S(2)}) copy-start(bf16[2,128,128,16]{1,0,3,2:T(2,128)(2,1)} %convert_element_type.71) | copy-start | bytes 3145732
  92.5 20.5 %slice-start = ((f32[2,128,128,16]{1,3,0,2:T(8,128)}), f32[1,128,128,16]{1,3,0,2:T(8,128)S(1)}, s32[]{:S(2)}) async-start(f32[2,128,128,16]{1,3,0,2:T(8,128)} %copy-done.1), calls=%async_computation | async-start | bytes 2097152 | tf_op jit(solution)/shard_map/slice | solution.py:60
  117.6 1.2 copy-start.2
  117.6 1.2 copy-start.3
  118.8 7.9 %copy-start.4 = (f32[2048]{0:T(1024)S(1)}, f32[2048]{0:T(1024)}, u32[]{:S(2)}) copy-start(f32[2048]{0:T(1024)} %param.11) | copy-start | bytes 24580
where the time goes:
time: 130 us
  local copies, waits for them, and re-layouts  72.3 us (56%)
  waiting for transfers between devices  19.4 us (15%)
  other arithmetic  16.1 us (12%)
  matrix products  9.33 us (7%)
  starting transfers between devices  6.23 us (5%)
  blocking collectives  6.22 us (5%)
    reshape x1, local copies, waits for them, and re-layouts, toeplitz(): return tiled.reshape(groups, filter_len, period - 1)[:, :, :2 * filter_len]  30.9 us
    unnamed x13, local copies, waits for them, and re-layouts  20.9 us
    ppermute x2, waiting for transfers between devices, passed_along(): return lax.ppermute(block, axis, route)  19.4 us
    convert_element_type x1, other arithmetic, featurize(): (weights[0] * padded[2:] + weights[1] * padded[1:-1] + weights[2] * padde...  10.5 us
    ppermute x2, starting transfers between devices, passed_along(): return lax.ppermute(block, axis, route)  6.23 us
    psum x1, blocking collectives, on_device(): lax.psum(jnp.sum(stream_f * stream_f, axis=1, keepdims=True), 'tp')  6.22 us
    another operation x1, local copies, waits for them, and re-layouts, toeplitz(): tiled = jnp.tile(pattern, (1, filter_len))[:, :filter_len * (period - 1)]  5.64 us
    slice x1, local copies, waits for them, and re-layouts, toeplitz(): tiled = jnp.tile(pattern, (1, filter_len))[:, :filter_len * (period - 1)]  5.12 us
  transfers between devices with their start and end apart: 2, of which 1 were waited for; matrix products, arithmetic and copies ran while one was open for 48% of the time, Pallas kernels for 0%

commit v1 on v0

v1 whole, which is shorter than its diff:
```python
import functools

import jax
import jax.numpy as jnp
from jax import lax
from jax.experimental import pallas as pl
from jax.experimental.pallas import tpu as pltpu
from jax.sharding import PartitionSpec as P

F32 = jnp.float32
BF16 = jnp.bfloat16
LANES = 128
HEAD = 80
TAIL = 48
EPS = 1e-06
HI = lax.Precision.HIGHEST
VMEM = pl.BlockSpec(memory_space=pltpu.VMEM)
MIB = 1 << 20


def causal3(x, w):
    return (w[0] * x + w[1] * pltpu.roll(x, 1, 0) + w[2] * pltpu.roll(x, 2, 0)).astype(BF16)


def tail_gate_kernel(kv_ref, q_ref, taps_ref, out_ref):
    halo = kv_ref.shape[1] - LANES
    key = kv_ref[0].astype(F32)
    val = kv_ref[1].astype(F32)
    k_feat = causal3(key, [taps_ref[s, 1:2] for s in range(3)])[halo:]
    v_feat = causal3(val, [taps_ref[s, 2:3] for s in range(3)])[halo:]
    out_ref[:LANES] = (k_feat.astype(F32) * v_feat.astype(F32)).astype(BF16)
    last_q = pltpu.roll(q_ref[0].astype(F32)[-8:], 2, 0)
    last_k = pltpu.roll(key[-8:], 4, 0)
    last_v = pltpu.roll(val[-8:], 6, 0)
    row = lax.broadcasted_iota(jnp.int32, last_q.shape, 0)
    rim = jnp.where(row < 2, last_q, jnp.where(row < 4, last_k, jnp.where(row < 6, last_v, 0.0)))
    out_ref[LANES:] = rim.astype(BF16)


def tail_gate(feats, short_taps):
    _, rows, channels = feats.shape
    width = channels // 4
    halo = 16
    return pl.pallas_call(
        tail_gate_kernel,
        grid=(channels // width,),
        in_specs=[
            pl.BlockSpec(
                (pl.Element(2), pl.Element(LANES + halo), pl.Element(width)),
                lambda i: (1, rows - LANES - halo, i * width),
            ),
            pl.BlockSpec(
                (pl.Element(1), pl.Element(16), pl.Element(width)),
                lambda i: (0, rows - 16, i * width),
            ),
            pl.BlockSpec((3, 3, width), lambda i: (0, 0, i)),
        ],
        out_specs=pl.BlockSpec((LANES + 8, width), lambda i: (0, i)),
        out_shape=jax.ShapeDtypeStruct((LANES + 8, channels), BF16),
        name="tail_gate",
    )(feats, feats, short_taps)


def group_select(prod, per_tile, rows):
    lane = lax.broadcasted_iota(jnp.int32, (rows, 2 * LANES), 1)
    owner = (lane % LANES) // (LANES // per_tile)
    acc = prod[:rows]
    for g in range(1, per_tile):
        acc = jnp.where(owner == g, prod[g * rows : (g + 1) * rows], acc)
    return jnp.concatenate([acc[:, :LANES], acc[:, LANES:]], 0)


def local_kernel(feats_ref, res_ref, short_ref, filt_ref, skip_ref, toep_ref, gate_ref, q_ref, stream_ref, ss_ref):
    tokens, channels = res_ref.shape
    tiles = channels // LANES
    per_tile = filt_ref.shape[0] // tiles
    first = tokens - 2 * TAIL
    tap = lax.broadcasted_iota(jnp.int32, (LANES, 2 * LANES), 0)
    pos = lax.broadcasted_iota(jnp.int32, (LANES, 2 * LANES), 1)
    flip = (tap + pos == LANES).astype(BF16)

    def tile(t, total):
        lanes = pl.ds(pl.multiple_of(t * LANES, LANES), LANES)
        feats = [
            causal3(feats_ref[s, :, lanes].astype(F32), [short_ref[i, s : s + 1, lanes] for i in range(3)])
            for s in range(3)
        ]
        gate = (feats[1].astype(F32) * feats[2].astype(F32)).astype(BF16)
        gate_ref[:, lanes] = gate
        q_ref[:, lanes] = feats[0]
        taps = filt_ref[pl.ds(pl.multiple_of(t * per_tile, per_tile), per_tile), :]
        base = jnp.dot(taps, flip, preferred_element_type=F32)
        lhs = []
        for g in range(per_tile):
            wide = jnp.broadcast_to(base[g : g + 1], (HEAD, 2 * LANES))
            band = pltpu.roll(wide, 0, 1, stride=1, stride_axis=0).astype(BF16)
            toep_ref[t, g * HEAD : (g + 1) * HEAD, :] = band
            lhs.append(band[:TAIL])
        z0 = jnp.zeros((first - LANES, LANES), BF16)
        z1 = jnp.zeros((first - LANES + TAIL, LANES), BF16)
        rhs = jnp.concatenate(
            [
                jnp.concatenate([gate[first - LANES :], z0], 0),
                jnp.concatenate([gate[first - LANES + TAIL :], z1], 0),
            ],
            1,
        )
        prod = jnp.dot(jnp.concatenate(lhs, 0), rhs, preferred_element_type=F32)
        filtered = group_select(prod, per_tile, TAIL)
        filtered = filtered + skip_ref[:, lanes] * gate[first:].astype(F32)
        stream = (res_ref[first:, lanes].astype(F32) + feats[0][first:].astype(F32) * filtered).astype(BF16)
        stream_ref[:, lanes] = stream
        wide_stream = stream.astype(F32)
        return total + wide_stream * wide_stream

    total = lax.fori_loop(0, tiles, tile, jnp.zeros((2 * TAIL, LANES), F32))
    ss_ref[...] = total


def local_part(feats, residual, short_taps, filter_taps, skip):
    _, tokens, channels = feats.shape
    tiles = channels // LANES
    per_tile = filter_taps.shape[0] // tiles
    return pl.pallas_call(
        local_kernel,
        in_specs=[VMEM] * 5,
        out_specs=[VMEM] * 5,
        out_shape=[
            jax.ShapeDtypeStruct((tiles, per_tile * HEAD, 2 * LANES), BF16),
            jax.ShapeDtypeStruct((tokens, channels), BF16),
            jax.ShapeDtypeStruct((tokens, channels), BF16),
            jax.ShapeDtypeStruct((2 * TAIL, channels), BF16),
            jax.ShapeDtypeStruct((2 * TAIL, LANES), F32),
        ],
        compiler_params=pltpu.CompilerParams(vmem_limit_bytes=48 * MIB),
        cost_estimate=pl.CostEstimate(flops=10**9, transcendentals=0, bytes_accessed=16 * MIB),
        name="local_part",
    )(feats, residual, short_taps, filter_taps, skip)


def head_kernel(carry_ref, feats_ref, res_ref, short_ref, skip_ref, toep_ref, gate_ref, q_ref, tail_ss_ref, stream_ref, ss_ref):
    channels = res_ref.shape[1]
    tiles = channels // LANES
    per_tile = toep_ref.shape[1] // HEAD
    rows = 2 * HEAD

    def tile(t, total):
        lanes = pl.ds(pl.multiple_of(t * LANES, LANES), LANES)
        rim = carry_ref[LANES:, lanes].astype(F32)
        row = lax.broadcasted_iota(jnp.int32, (16, LANES), 0)
        feats = []
        for s in range(3):
            x = feats_ref[s, :16, lanes].astype(F32)
            w = [short_ref[i, s : s + 1, lanes] for i in range(3)]
            older, newer = rim[2 * s : 2 * s + 1], rim[2 * s + 1 : 2 * s + 2]
            x1 = jnp.where(row == 0, newer, pltpu.roll(x, 1, 0))
            x2 = jnp.where(row == 0, older, jnp.where(row == 1, newer, pltpu.roll(x, 2, 0)))
            feats.append((w[0] * x + w[1] * x1 + w[2] * x2).astype(BF16))
        fixed = (feats[1].astype(F32) * feats[2].astype(F32)).astype(BF16)
        gate = jnp.concatenate([fixed, gate_ref[16 : 2 * LANES - LANES + HEAD, lanes]], 0)
        query = jnp.concatenate([feats[0], q_ref[16:rows, lanes]], 0)
        carry = carry_ref[:LANES, lanes]
        rhs = jnp.concatenate(
            [
                jnp.concatenate([carry, gate[:LANES]], 0),
                jnp.concatenate([carry[HEAD:], gate[: LANES + HEAD]], 0),
            ],
            1,
        )
        prod = jnp.dot(toep_ref[t], rhs, preferred_element_type=F32)
        filtered = group_select(prod, per_tile, HEAD)
        filtered = filtered + skip_ref[:, lanes] * gate[:rows].astype(F32)
        stream = (res_ref[:rows, lanes].astype(F32) + query.astype(F32) * filtered).astype(BF16)
        stream_ref[:, lanes] = stream
        wide_stream = stream.astype(F32)
        return total + wide_stream * wide_stream

    total = lax.fori_loop(0, tiles, tile, jnp.zeros((rows, LANES), F32))
    total = jnp.concatenate([total, tail_ss_ref[...]], 0)
    ones = jnp.ones((8, LANES), F32)
    ss_ref[...] = lax.dot_general(
        ones, total, (((1,), (1,)), ((), ())), precision=HI, preferred_element_type=F32
    )


def head_part(carry, feats, residual, short_taps, skip, toep, gate, query, tail_ss):
    tokens, channels = residual.shape
    return pl.pallas_call(
        head_kernel,
        in_specs=[VMEM] * 9,
        out_specs=[VMEM] * 2,
        out_shape=[
            jax.ShapeDtypeStruct((2 * HEAD, channels), BF16),
            jax.ShapeDtypeStruct((8, tokens), F32),
        ],
        compiler_params=pltpu.CompilerParams(vmem_limit_bytes=48 * MIB),
        name="head_part",
    )(carry, feats, residual, short_taps, skip, toep, gate, query, tail_ss)


def norm_kernel(width, ss_ref, head_ref, tail_ref, gain_ref, out_ref):
    ones = jnp.ones((ss_ref.shape[0], LANES), F32)
    sums = lax.dot_general(
        ss_ref[...], ones, (((0,), (0,)), ((), ())), precision=HI, preferred_element_type=F32
    )
    scale = lax.rsqrt(sums / width + EPS)
    split = head_ref.shape[0]
    for t in range(head_ref.shape[1] // LANES):
        lanes = slice(t * LANES, (t + 1) * LANES)
        out_ref[:split, lanes] = (head_ref[:, lanes].astype(F32) * scale[:split] * gain_ref[:, lanes]).astype(BF16)
        out_ref[split:, lanes] = (tail_ref[:, lanes].astype(F32) * scale[split:] * gain_ref[:, lanes]).astype(BF16)


def normalize(ss, head, tail, gain, width):
    tokens = head.shape[0] + tail.shape[0]
    channels = head.shape[1]
    return pl.pallas_call(
        functools.partial(norm_kernel, width),
        in_specs=[VMEM] * 4,
        out_specs=VMEM,
        out_shape=jax.ShapeDtypeStruct((tokens, channels), BF16),
        compiler_params=pltpu.CompilerParams(vmem_limit_bytes=48 * MIB),
        name="normalize",
    )(ss, head, tail, gain)


def on_device(residual, features, short_taps, filter_taps, skip_gain, norm_gain):
    channels = residual.shape[1]
    feats = jnp.transpose(features, (1, 0, 2))
    skip = skip_gain.reshape(1, channels)
    gain = norm_gain.reshape(1, channels)
    sent = tail_gate(feats, short_taps)
    size = lax.axis_size("ctx")
    carry = lax.ppermute(sent, "ctx", [(i, i + 1) for i in range(size - 1)])
    toep, gate, query, tail, tail_ss = local_part(feats, residual, short_taps, filter_taps, skip)
    head, ss = head_part(carry, feats, residual, short_taps, skip, toep, gate, query, tail_ss)
    ss = lax.all_gather(ss[0], "tp")
    return normalize(ss, head, tail, gain, channels * lax.axis_size("tp"))


def solution(mesh):
    in_specs = (
        P("ctx", "tp"),
        P("ctx", None, "tp"),
        P(None, None, "tp"),
        P("tp", None),
        P("tp"),
        P("tp"),
    )
    return jax.shard_map(
        on_device, mesh=mesh, in_specs=in_specs, out_specs=P("ctx", "tp"), check_vma=False
    )
```

time: 130 us -> 46.6 us (0.36)
  local copies, waits for them, and re-layouts: 72.3 us -> 0.02 us
  Pallas kernels: 0 us -> 24.9 us
  other arithmetic: 16.1 us -> 0 us
  matrix products: 9.33 us -> 0 us
  waiting for transfers between devices: 19.4 us -> 12.2 us
  starting transfers between devices: 6.23 us -> 3.11 us
    reshape x1 -> x0, local copies, waits for them, and re-layouts: 30.9 us -> none  [toeplitz(): return tiled.reshape(groups, filter_len, period - 1)[:, :, :2 * filter_len]]
    pallas_call x0 -> x4, Pallas kernels: none -> 24.9 us  [the longest x1 11.2 us: local_part(): pl.pallas_call(local_kernel, in_specs=[VMEM] * 5, out_specs=[VMEM] * 5, o...]
    unnamed x13 -> x12, local copies, waits for them, and re-layouts: 20.9 us -> 0.02 us
    convert_element_type x3 -> x0, other arithmetic: 13.2 us -> none  [the longest x1 10.5 us: featurize(): (weights[0] * padded[2:] + weights[1] * padded[1:-1] + weights[2] * padde...]
    dot_general x2 -> x0, matrix products: 9.33 us -> none  [the longest x1 4.79 us: on_device(): jnp.einsum('gij,bjgs->bigs', upper_band, stacked, preferred_element_type=...]
    ppermute x2 -> x1, waiting for transfers between devices: 19.4 us -> 12.2 us  [on_device(): carry = lax.ppermute(sent, 'ctx', [(i, i + 1) for i in range(size - 1)])]
    psum x1 -> x0, blocking collectives: 6.22 us -> none  [on_device(): lax.psum(jnp.sum(stream_f * stream_f, axis=1, keepdims=True), 'tp')]
    all_gather x0 -> x1, blocking collectives: none -> 6.08 us  [on_device(): ss = lax.all_gather(ss[0], 'tp')]
  transfers between devices with their start and end apart: 2 -> 1, of which waited for: 1 -> 1; matrix products, arithmetic and copies ran while one was open for 48% -> 0% of each run, Pallas kernels for 0% -> 24%
where the time goes in v1:
time: 46.6 us; the launch traced here: 46.4 us
  Pallas kernels  24.9 us (53%)
  waiting for transfers between devices  12.2 us (26%)
  blocking collectives  6.08 us (13%)
  starting transfers between devices  3.11 us (7%)
    ppermute x1, waiting for transfers between devices, on_device(): carry = lax.ppermute(sent, 'ctx', [(i, i + 1) for i in range(size - 1)])  12.2 us
    pallas_call x1, Pallas kernels, local_part(): pl.pallas_call(local_kernel, in_specs=[VMEM] * 5, out_specs=[VMEM] * 5, o...  11.2 us
    pallas_call x1, Pallas kernels, head_part(): pl.pallas_call(head_kernel, in_specs=[VMEM] * 9, out_specs=[VMEM] * 2, ou...  8.28 us
    all_gather x1, blocking collectives, on_device(): ss = lax.all_gather(ss[0], 'tp')  6.08 us
    pallas_call x1, Pallas kernels, tail_gate(): pl.pallas_call(tail_gate_kernel, grid=(channels // width,), in_specs=[pl....  3.85 us
    ppermute x1, starting transfers between devices, on_device(): carry = lax.ppermute(sent, 'ctx', [(i, i + 1) for i in range(size - 1)])  3.11 us
    pallas_call x1, Pallas kernels, normalize(): pl.pallas_call(functools.partial(norm_kernel, width), in_specs=[VMEM] * 4...  1.59 us
  transfers between devices with their start and end apart: 1, of which 1 were waited for; matrix products, arithmetic and copies ran while one was open for 0% of the time, Pallas kernels for 24%

profile of v1, /device:TPU:25, one launch (start us, length us, event | category | flops | bytes accessed | tf_op | source)
XLA Modules:
  0.0 46.4 jit_solution(4520921933040675675)
XLA Ops:
  0.0 0.0 copy-start.1
  0.0 0.0 copy-start
  0.0 0.0 copy-start.3
  0.0 0.0 copy-start.2
  0.0 3.8 %tail_gate.1 = bf16[136,2048]{1,0:T(8,128)(2,1)} custom-call(bf16[3,256,2048]{2,1,0:T(8,128)(2,1)} %bitcast.12, bf16[3,256,2048]{2,1,0:T(8,128)(2,1)} %bitcast.13, f32[3,3,2048]{2,1,0:T(4,128)} %short_ref.3), custom_call_target="tpu_custom_call" | custom-call | tf_op jit(solution)/shard_map/tail_gate/pallas_call | solution.py:44
  3.9 3.1 %collective-permute-start = (bf16[136,2048]{1,0:T(8,128)(2,1)}, bf16[136,2048]{1,0:T(8,128)(2,1)S(1)}, u32[]{:S(2)}, u32[]{:S(2)}) collective-permute-start(bf16[136,2048]{1,0:T(8,128)(2,1)} %tail_gate.1), channel_id=1, source_target_pairs={{0,4},{4,8},{8,12},{12,16},{16,20},{20,24},{24,28},{28,32},{32,36}... | collective-permute-start | bytes 1671176 | tf_op jit(solution)/shard_map/ppermute | solution.py:234
  7.0 0.0 copy-done.1
  7.0 0.0 copy-done
  7.0 0.0 copy-done.3
  7.0 0.0 copy-done.2
  7.0 11.2 %local_part.1 = (bf16[16,640,256]{2,1,0:T(8,128)(2,1)}, bf16[256,2048]{1,0:T(8,128)(2,1)S(1)}, bf16[256,2048]{1,0:T(8,128)(2,1)S(1)}, bf16[96,2048]{1,0:T(8,128)(2,1)S(1)}, f32[96,128]{1,0:T(8,128)S(1)}) custom-call(bf16[3,256,2048]{2,1,0:T(8,128)(2,1)} %bitcast.14, bf16[256,2048]{1,0:T(8,128)(2,1)S(1)} %copy-done, f32[3,3,2048]{2,1,0:T(4,128)S(1)} %copy-done.1, ...), custom_call_target="tpu_custom_call" | custom-call | flops 1000000000 | bytes 16777216 | tf_op jit(solution)/shard_map/local_part/pallas_call | solution.py:124
  18.2 12.2 %collective-permute-done.carry_ref = bf16[136,2048]{1,0:T(8,128)(2,1)S(1)} collective-permute-done((bf16[136,2048]{1,0:T(8,128)(2,1)}, bf16[136,2048]{1,0:T(8,128)(2,1)S(1)}, u32[]{:S(2)}, u32[]{:S(2)}) %collective-permute-start) | collective-permute-done | bytes 557088 | tf_op jit(solution)/shard_map/ppermute | solution.py:234
  30.4 0.0 copy-start.4
  30.4 8.3 %head_part.1 = (bf16[160,2048]{1,0:T(8,128)(2,1)S(1)}, f32[8,256]{1,0:T(8,128)S(1)}) custom-call(bf16[136,2048]{1,0:T(8,128)(2,1)S(1)} %collective-permute-done.carry_ref, bf16[3,256,2048]{2,1,0:T(8,128)(2,1)} %bitcast.15, bf16[256,2048]{1,0:T(8,128)(2,1)S(1)} %copy-done, f32[3,3,2048]{2,1,0:T(4,128)S(1)} %copy-done.1, f32[1,2048]{1,0:T(1,128)S(1)} %bitcast.9, ...), custom_call_target="tpu_custom_call" | custom-call | tf_op jit(solution)/shard_map/head_part/pallas_call | solution.py:188
  38.7 6.1 %all-gather = f32[4,1,256]{2,1,0:T(1,128)S(1)} all-gather(f32[1,1,256]{2,1,0:T(1,128)S(1)} %slice_bitcast_fusion), channel_id=1, replica_groups=mesh['ctx'=128,'tp'=4] {'tp'}, dimensions={0}, use_global_device_ids=true | all-gather | bytes 5120 | tf_op jit(solution)/shard_map/all_gather | solution.py:237
  44.8 0.0 copy-done.4
  44.8 1.6 %normalize.1 = bf16[256,2048]{1,0:T(8,128)(2,1)} custom-call(f32[4,256]{1,0:T(4,128)S(1)} %bitcast.10, bf16[160,2048]{1,0:T(8,128)(2,1)S(1)} %get-tuple-element.17.head_ref, bf16[96,2048]{1,0:T(8,128)(2,1)S(1)} %get-tuple-element.18.tail_ref, f32[1,2048]{1,0:T(1,128)S(1)} %bitcast.11), custom_call_target="tpu_custom_call" | custom-call | tf_op jit(solution)/shard_map/normalize/pallas_call | solution.py:217
  (2 shorter events, 0.0 us)
Async XLA Ops:
  0.0 7.0 %copy-start.1 = (f32[3,3,2048]{2,1,0:T(4,128)S(1)}, f32[3,3,2048]{2,1,0:T(4,128)}, u32[]{:S(2)}) copy-start(f32[3,3,2048]{2,1,0:T(4,128)} %short_ref.3) | copy-start | bytes 221188
  0.0 7.0 %copy-start = (bf16[256,2048]{1,0:T(8,128)(2,1)S(1)}, bf16[256,2048]{1,0:T(8,128)(2,1)}, u32[]{:S(2)}) copy-start(bf16[256,2048]{1,0:T(8,128)(2,1)} %res_ref.3) | copy-start | bytes 3145732
  0.0 7.0 %copy-start.3 = (f32[2048]{0:T(1024)S(1)}, f32[2048]{0:T(1024)}, u32[]{:S(2)}) copy-start(f32[2048]{0:T(1024)} %param.10) | copy-start | bytes 24580
  0.0 7.0 %copy-start.2 = (bf16[128,128]{1,0:T(8,128)(2,1)S(1)}, bf16[128,128]{1,0:T(8,128)(2,1)}, u32[]{:S(2)}) copy-start(bf16[128,128]{1,0:T(8,128)(2,1)} %filt_ref.1) | copy-start | bytes 98308
  3.9 26.5 %collective-permute-start = (bf16[136,2048]{1,0:T(8,128)(2,1)}, bf16[136,2048]{1,0:T(8,128)(2,1)S(1)}, u32[]{:S(2)}, u32[]{:S(2)}) collective-permute-start(bf16[136,2048]{1,0:T(8,128)(2,1)} %tail_gate.1), channel_id=1, source_target_pairs={{0,4},{4,8},{8,12},{12,16},{16,20},{20,24},{24,28},{28,32},{32,36}... | collective-permute-start | bytes 1671176 | tf_op jit(solution)/shard_map/ppermute | solution.py:234
  30.4 14.4 %copy-start.4 = (f32[2048]{0:T(1024)S(1)}, f32[2048]{0:T(1024)}, u32[]{:S(2)}) copy-start(f32[2048]{0:T(1024)} %param.11) | copy-start | bytes 24580

commit v2 on v1

v2 whole, which is shorter than its diff:
```python
import functools

import jax
import jax.numpy as jnp
from jax import lax
from jax.experimental import pallas as pl
from jax.experimental.pallas import tpu as pltpu
from jax.sharding import PartitionSpec as P

F32 = jnp.float32
BF16 = jnp.bfloat16
LANES = 128
HEAD = 80
TAIL = 48
EPS = 1e-06
WIDTHS = (768, 768, 512)
UNROLL = 2
NORM_BLOCKS = 4
VMEM = pl.BlockSpec(memory_space=pltpu.VMEM)
MIB = 1 << 20


def in_hbm(x):
    return pltpu.with_memory_space_constraint(x, pltpu.HBM)


def causal3(x, w):
    return w[0] * x + w[1] * pltpu.roll(x, 1, 0) + w[2] * pltpu.roll(x, 2, 0)


def gate_tile(load_kv, last_q, taps, halo):
    raw = [load_kv(s).astype(F32) for s in range(2)]
    feat = [causal3(raw[s], taps[s])[halo:] for s in range(2)]
    gate = (feat[0] * feat[1]).astype(BF16)
    last_q = pltpu.roll(last_q.astype(F32)[-8:], 2, 0)
    last_k = pltpu.roll(raw[0][-8:], 4, 0)
    last_v = pltpu.roll(raw[1][-8:], 6, 0)
    row = lax.broadcasted_iota(jnp.int32, last_q.shape, 0)
    rim = jnp.where(row < 2, last_q, jnp.where(row < 4, last_k, jnp.where(row < 6, last_v, 0.0)))
    return gate, rim.astype(BF16)


def tail_gate_kernel(begin, feats_ref, short_ref, out_ref, kv_ref, q_ref, taps_ref, sem):
    rows = feats_ref.shape[1]
    width = out_ref.shape[1]
    halo = kv_ref.shape[1] - LANES
    here = pl.ds(begin, width)
    copies = [
        pltpu.make_async_copy(feats_ref.at[pl.ds(1, 2), pl.ds(rows - LANES - halo, LANES + halo), here], kv_ref, sem.at[0]),
        pltpu.make_async_copy(feats_ref.at[0, pl.ds(rows - 16, 16), here], q_ref, sem.at[1]),
        pltpu.make_async_copy(short_ref.at[:, :, here], taps_ref, sem.at[2]),
    ]
    for copy in copies:
        copy.start()
    for copy in copies:
        copy.wait()
    for t in range(width // LANES):
        lanes = slice(t * LANES, (t + 1) * LANES)
        taps = [[taps_ref[i, s : s + 1, lanes] for i in range(3)] for s in (1, 2)]
        gate, rim = gate_tile(lambda s: kv_ref[s, :, lanes], q_ref[:, lanes], taps, halo)
        out_ref[:LANES, lanes] = gate
        out_ref[LANES:, lanes] = rim


def tail_gate(feats, short_taps, begin, width):
    halo = 16
    return pl.pallas_call(
        functools.partial(tail_gate_kernel, begin),
        in_specs=[pl.BlockSpec(memory_space=pltpu.HBM)] * 2,
        out_specs=VMEM,
        out_shape=jax.ShapeDtypeStruct((LANES + 8, width), BF16),
        scratch_shapes=[
            pltpu.VMEM((2, LANES + halo, width), BF16),
            pltpu.VMEM((16, width), BF16),
            pltpu.VMEM((3, 3, width), F32),
            pltpu.SemaphoreType.DMA((3,)),
        ],
        compiler_params=pltpu.CompilerParams(vmem_limit_bytes=4 * MIB),
        name="tail_gate",
    )(in_hbm(feats), in_hbm(short_taps))


def group_select(prod, per_tile, rows):
    lane = lax.broadcasted_iota(jnp.int32, (rows, 2 * LANES), 1)
    owner = (lane % LANES) // (LANES // per_tile)
    acc = prod[:rows]
    for g in range(1, per_tile):
        acc = jnp.where(owner == g, prod[g * rows : (g + 1) * rows], acc)
    return jnp.concatenate([acc[:, :LANES], acc[:, LANES:]], 0)


def local_kernel(
    hbm_ref, res_ref, short_ref, filt_ref, skip_ref, toep_ref, gate_ref, q_ref, first_ref, stream_ref, ss_ref, feats_ref, sem
):
    tokens, channels = res_ref.shape
    part = UNROLL * LANES

    def load(p):
        lanes = pl.ds(pl.multiple_of(p * part, part), part)
        return pltpu.make_async_copy(hbm_ref.at[:, :, lanes], feats_ref.at[:, :, lanes], sem.at[p])

    for p in range(channels // part):
        load(p).start()
    tiles = channels // LANES
    per_tile = filt_ref.shape[0] // tiles
    first = tokens - 2 * TAIL
    tap = lax.broadcasted_iota(jnp.int32, (LANES, 2 * LANES), 0)
    pos = lax.broadcasted_iota(jnp.int32, (LANES, 2 * LANES), 1)
    flip = (tap + pos == LANES).astype(BF16)

    def tile(t):
        lanes = pl.ds(pl.multiple_of(t * LANES, LANES), LANES)
        first_ref[:, :, lanes] = feats_ref[:, : first_ref.shape[1], lanes]
        feats = [
            causal3(feats_ref[s, :, lanes].astype(F32), [short_ref[i, s : s + 1, lanes] for i in range(3)])
            for s in range(3)
        ]
        gate = (feats[1] * feats[2]).astype(BF16)
        gate_ref[:, lanes] = gate
        q_ref[:, lanes] = feats[0].astype(BF16)
        taps = filt_ref[pl.ds(pl.multiple_of(t * per_tile, per_tile), per_tile), :]
        base = jnp.dot(taps, flip, preferred_element_type=F32)
        lhs = []
        for g in range(per_tile):
            wide = jnp.broadcast_to(base[g : g + 1], (HEAD, 2 * LANES))
            band = pltpu.roll(wide, 0, 1, stride=1, stride_axis=0).astype(BF16)
            toep_ref[t, g * HEAD : (g + 1) * HEAD, :] = band
            lhs.append(band[:TAIL])
        z0 = jnp.zeros((first - LANES, LANES), BF16)
        z1 = jnp.zeros((first - LANES + TAIL, LANES), BF16)
        rhs = jnp.concatenate(
            [
                jnp.concatenate([gate[first - LANES :], z0], 0),
                jnp.concatenate([gate[first - LANES + TAIL :], z1], 0),
            ],
            1,
        )
        prod = jnp.dot(jnp.concatenate(lhs, 0), rhs, preferred_element_type=F32)
        filtered = group_select(prod, per_tile, TAIL)
        filtered = filtered + skip_ref[:, lanes] * gate[first:].astype(F32)
        stream = (res_ref[first:, lanes].astype(F32) + feats[0][first:] * filtered).astype(BF16)
        stream_ref[:, lanes] = stream
        wide_stream = stream.astype(F32)
        return wide_stream * wide_stream

    def step(p, total):
        load(p).wait()
        for u in range(UNROLL):
            total = total + tile(p * UNROLL + u)
        return total

    ss_ref[...] = lax.fori_loop(0, tiles // UNROLL, step, jnp.zeros((2 * TAIL, LANES), F32))


def local_part(feats, residual, short_taps, filter_taps, skip):
    _, tokens, channels = feats.shape
    tiles = channels // LANES
    per_tile = filter_taps.shape[0] // tiles
    return pl.pallas_call(
        local_kernel,
        in_specs=[pl.BlockSpec(memory_space=pltpu.HBM)] + [VMEM] * 4,
        out_specs=[VMEM] * 6,
        out_shape=[
            jax.ShapeDtypeStruct((tiles, per_tile * HEAD, 2 * LANES), BF16),
            jax.ShapeDtypeStruct((tokens, channels), BF16),
            jax.ShapeDtypeStruct((tokens, channels), BF16),
            jax.ShapeDtypeStruct((3, 16, channels), BF16),
            jax.ShapeDtypeStruct((2 * TAIL, channels), BF16),
            jax.ShapeDtypeStruct((2 * TAIL, LANES), F32),
        ],
        scratch_shapes=[
            pltpu.VMEM(feats.shape, BF16),
            pltpu.SemaphoreType.DMA((channels // (UNROLL * LANES),)),
        ],
        compiler_params=pltpu.CompilerParams(vmem_limit_bytes=16 * MIB),
        cost_estimate=pl.CostEstimate(flops=10**9, transcendentals=0, bytes_accessed=16 * MIB),
        name="local_part",
    )(in_hbm(feats), residual, short_taps, filter_taps, skip)


def head_kernel(start, carry_ref, first_ref, res_ref, short_ref, skip_ref, toep_ref, gate_ref, q_ref, before_ref, stream_ref, ss_ref):
    per_tile = toep_ref.shape[1] // HEAD
    rows = 2 * HEAD
    row = lax.broadcasted_iota(jnp.int32, (16, LANES), 0)
    total = before_ref[-rows:] if before_ref.shape[0] >= rows else jnp.zeros((rows, LANES), F32)
    for c in range(carry_ref.shape[1] // LANES):
        near = slice(c * LANES, (c + 1) * LANES)
        lanes = slice(start + c * LANES, start + (c + 1) * LANES)
        rim = carry_ref[LANES:, near].astype(F32)
        carry = carry_ref[:LANES, near]
        feats = []
        for s in range(3):
            x = first_ref[s, :, lanes].astype(F32)
            w = [short_ref[i, s : s + 1, lanes] for i in range(3)]
            older, newer = rim[2 * s : 2 * s + 1], rim[2 * s + 1 : 2 * s + 2]
            x1 = jnp.where(row == 0, newer, pltpu.roll(x, 1, 0))
            x2 = jnp.where(row == 0, older, jnp.where(row == 1, newer, pltpu.roll(x, 2, 0)))
            feats.append(w[0] * x + w[1] * x1 + w[2] * x2)
        fixed = (feats[1] * feats[2]).astype(BF16)
        gate = jnp.concatenate([fixed, gate_ref[16 : LANES + HEAD, lanes]], 0)
        query = jnp.concatenate([feats[0].astype(BF16), q_ref[16:rows, lanes]], 0)
        rhs = jnp.concatenate(
            [jnp.concatenate([carry, gate[:LANES]], 0), jnp.concatenate([carry[HEAD:], gate], 0)], 1
        )
        prod = jnp.dot(toep_ref[start // LANES + c], rhs, preferred_element_type=F32)
        filtered = group_select(prod, per_tile, HEAD)
        filtered = filtered + skip_ref[:, lanes] * gate[:rows].astype(F32)
        stream = (res_ref[:rows, lanes].astype(F32) + query.astype(F32) * filtered).astype(BF16)
        stream_ref[:, near] = stream
        wide_stream = stream.astype(F32)
        total = total + wide_stream * wide_stream
    if ss_ref.shape[0] == 8:
        total = jnp.concatenate([total, before_ref[: 2 * TAIL]], 0)
        sums = jnp.sum(jnp.transpose(total), axis=0, keepdims=True)
        ss_ref[...] = jnp.broadcast_to(sums, ss_ref.shape)
    else:
        ss_ref[: 2 * TAIL] = before_ref[: 2 * TAIL]
        ss_ref[2 * TAIL :] = total


def head_part(start, last, carry, first, residual, short_taps, skip, toep, gate, query, before):
    tokens = residual.shape[0]
    ss_shape = (8, tokens) if last else (tokens, LANES)
    return pl.pallas_call(
        functools.partial(head_kernel, start),
        in_specs=[VMEM] * 9,
        out_specs=[VMEM] * 2,
        out_shape=[
            jax.ShapeDtypeStruct((2 * HEAD, carry.shape[1]), BF16),
            jax.ShapeDtypeStruct(ss_shape, F32),
        ],
        compiler_params=pltpu.CompilerParams(vmem_limit_bytes=8 * MIB),
        name="head_part",
    )(carry, first, residual, short_taps, skip, toep, gate, query, before)


def norm_kernel(width, ss_ref, *refs):
    *head_refs, tail_ref, gain_ref, out_ref, buf, sem = refs
    tokens = buf.shape[0]
    split = head_refs[0].shape[0]
    sums = jnp.sum(ss_ref[...], axis=0, keepdims=True)
    scale = jnp.transpose(jnp.broadcast_to(lax.rsqrt(sums / width + EPS), (LANES, tokens)))
    copies = []
    step = tokens // NORM_BLOCKS
    for b in range(NORM_BLOCKS):
        begin, end = b * step, (b + 1) * step
        for low, high, offset, refs_here in (
            (begin, min(end, split), 0, head_refs),
            (max(begin, split), end, split, [tail_ref]),
        ):
            if high <= low:
                continue
            base = 0
            for ref in refs_here:
                for t in range(ref.shape[1] // LANES):
                    near = slice(t * LANES, (t + 1) * LANES)
                    lanes = slice(base + t * LANES, base + (t + 1) * LANES)
                    value = ref[low - offset : high - offset, near].astype(F32)
                    buf[low:high, lanes] = (value * scale[low:high] * gain_ref[:, lanes]).astype(BF16)
                base += ref.shape[1]
        copy = pltpu.make_async_copy(buf.at[begin:end], out_ref.at[begin:end], sem.at[b])
        copy.start()
        copies.append(copy)
    for copy in copies:
        copy.wait()


def normalize(ss, heads, tail, gain, width):
    tokens = heads[0].shape[0] + tail.shape[0]
    channels = tail.shape[1]
    return pl.pallas_call(
        functools.partial(norm_kernel, width),
        in_specs=[VMEM] * (3 + len(heads)),
        out_specs=pl.BlockSpec(memory_space=pl.ANY),
        out_shape=jax.ShapeDtypeStruct((tokens, channels), BF16),
        scratch_shapes=[pltpu.VMEM((tokens, channels), BF16), pltpu.SemaphoreType.DMA((NORM_BLOCKS,))],
        compiler_params=pltpu.CompilerParams(vmem_limit_bytes=8 * MIB),
        name="normalize",
    )(ss, *heads, tail, gain)


def on_device(residual, features, short_taps, filter_taps, skip_gain, norm_gain):
    channels = residual.shape[1]
    feats = jnp.transpose(features, (1, 0, 2))
    skip = skip_gain.reshape(1, channels)
    gain = norm_gain.reshape(1, channels)
    size = lax.axis_size("ctx")
    route = [(i, i + 1) for i in range(size - 1)]
    starts = [sum(WIDTHS[:i]) for i in range(len(WIDTHS))]
    parts = [tail_gate(feats, short_taps, s, w) for s, w in zip(starts, WIDTHS)]
    carries = [lax.ppermute(part, "ctx", route) for part in parts]
    toep, gate, query, first, tail, ss = local_part(feats, residual, short_taps, filter_taps, skip)
    heads = []
    for start, carry in zip(starts, carries):
        last = start + carry.shape[1] == channels
        head, ss = head_part(start, last, carry, first, residual, short_taps, skip, toep, gate, query, ss)
        heads.append(head)
    ss = lax.all_gather(ss[0], "tp")
    return normalize(ss, heads, tail, gain, channels * lax.axis_size("tp"))


def solution(mesh):
    in_specs = (
        P("ctx", "tp"),
        P("ctx", None, "tp"),
        P(None, None, "tp"),
        P("tp", None),
        P("tp"),
        P("tp"),
    )
    return jax.shard_map(
        on_device, mesh=mesh, in_specs=in_specs, out_specs=P("ctx", "tp"), check_vma=False
    )
```

time: 46.6 us -> 36.1 us (0.77)
  Pallas kernels: 24.9 us -> 13.9 us
  starting transfers between devices: 3.11 us -> 9.06 us
  waiting for transfers between devices: 12.2 us -> 6.62 us
    pallas_call x4 -> x8, Pallas kernels: 24.9 us -> 13.9 us  [the longest x1 6.4 us: local_part(): pl.pallas_call(local_kernel, in_specs=[pl.BlockSpec(memory_space=pltpu.HB...]
    ppermute x1 -> x3, starting transfers between devices: 3.11 us -> 9.06 us  [on_device(): carries = [lax.ppermute(part, 'ctx', route) for part in parts]]
    ppermute x1 -> x3, waiting for transfers between devices: 12.2 us -> 6.62 us  [on_device(): carries = [lax.ppermute(part, 'ctx', route) for part in parts]]
  transfers between devices with their start and end apart: 1 -> 3, of which waited for: 1 -> 3; matrix products, arithmetic and copies ran while one was open for 0% -> 0% of each run, Pallas kernels for 24% -> 29%
where the time goes in v2:
time: 36.1 us; the launch traced here: 35.9 us
  Pallas kernels  13.9 us (39%)
  starting transfers between devices  9.06 us (25%)
  waiting for transfers between devices  6.62 us (18%)
  blocking collectives  6.13 us (17%)
    ppermute x3, starting transfers between devices, on_device(): carries = [lax.ppermute(part, 'ctx', route) for part in parts]  9.06 us
    ppermute x3, waiting for transfers between devices, on_device(): carries = [lax.ppermute(part, 'ctx', route) for part in parts]  6.62 us
    pallas_call x1, Pallas kernels, local_part(): pl.pallas_call(local_kernel, in_specs=[pl.BlockSpec(memory_space=pltpu.HB...  6.4 us
    all_gather x1, blocking collectives, on_device(): ss = lax.all_gather(ss[0], 'tp')  6.13 us
    pallas_call x3, Pallas kernels, tail_gate(): pl.pallas_call(functools.partial(tail_gate_kernel, begin), in_specs=[pl.B...  3.99 us
    pallas_call x3, Pallas kernels, head_part(): pl.pallas_call(functools.partial(head_kernel, start), in_specs=[VMEM] * 9...  2.25 us
    pallas_call x1, Pallas kernels, normalize(): pl.pallas_call(functools.partial(norm_kernel, width), in_specs=[VMEM] * (...  1.23 us
  transfers between devices with their start and end apart: 3, of which 3 were waited for; matrix products, arithmetic and copies ran while one was open for 0% of the time, Pallas kernels for 29%

profile of v2, /device:TPU:25, one launch (start us, length us, event | category | flops | bytes accessed | tf_op | source)
XLA Modules:
  0.0 35.9 jit_solution(2326724133716050565)
XLA Ops:
  0.0 0.0 copy-start.1
  0.0 0.0 copy-start.2
  0.0 0.0 copy-start
  0.0 0.0 copy-start.3
  0.0 1.4 %tail_gate.5 = bf16[136,768]{1,0:T(8,128)(2,1)S(1)} custom-call(bf16[3,256,2048]{2,1,0:T(8,128)(2,1)} %bitcast.14, f32[3,3,2048]{2,1,0:T(4,128)} %short_ref.13), custom_call_target="tpu_custom_call" | custom-call | tf_op jit(solution)/shard_map/tail_gate/pallas_call | solution.py:67
  1.5 3.1 %collective-permute-start.2 = (bf16[136,768]{1,0:T(8,128)(2,1)S(1)}, bf16[136,768]{1,0:T(8,128)(2,1)S(1)}, u32[]{:S(2)}, u32[]{:S(2)}) collective-permute-start(bf16[136,768]{1,0:T(8,128)(2,1)S(1)} %tail_gate.5), channel_id=1, source_target_pairs={{0,4},{4,8},{8,12},{12,16},{16,20},{20,24},{24,28},{28,32},{32,36}... | collective-permute-start | bytes 626696 | tf_op jit(solution)/shard_map/ppermute | solution.py:291
  4.6 1.3 %tail_gate.4 = bf16[136,768]{1,0:T(8,128)(2,1)S(1)} custom-call(bf16[3,256,2048]{2,1,0:T(8,128)(2,1)} %bitcast.15, f32[3,3,2048]{2,1,0:T(4,128)} %short_ref.13), custom_call_target="tpu_custom_call" | custom-call | tf_op jit(solution)/shard_map/tail_gate/pallas_call | solution.py:67
  6.0 3.1 %collective-permute-start.1 = (bf16[136,768]{1,0:T(8,128)(2,1)S(1)}, bf16[136,768]{1,0:T(8,128)(2,1)S(1)}, u32[]{:S(2)}, u32[]{:S(2)}) collective-permute-start(bf16[136,768]{1,0:T(8,128)(2,1)S(1)} %tail_gate.4), channel_id=1, source_target_pairs={{0,4},{4,8},{8,12},{12,16},{16,20},{20,24},{24,28},{28,32},{32,36}... | collective-permute-start | bytes 626696 | tf_op jit(solution)/shard_map/ppermute | solution.py:291
  9.1 1.2 %tail_gate.3 = bf16[136,512]{1,0:T(8,128)(2,1)S(1)} custom-call(bf16[3,256,2048]{2,1,0:T(8,128)(2,1)} %bitcast.16, f32[3,3,2048]{2,1,0:T(4,128)} %short_ref.13), custom_call_target="tpu_custom_call" | custom-call | tf_op jit(solution)/shard_map/tail_gate/pallas_call | solution.py:67
  10.3 2.8 %collective-permute-start = (bf16[136,512]{1,0:T(8,128)(2,1)S(1)}, bf16[136,512]{1,0:T(8,128)(2,1)S(1)}, u32[]{:S(2)}, u32[]{:S(2)}) collective-permute-start(bf16[136,512]{1,0:T(8,128)(2,1)S(1)} %tail_gate.3), channel_id=1, source_target_pairs={{0,4},{4,8},{8,12},{12,16},{16,20},{20,24},{24,28},{28,32},{32,36}... | collective-permute-start | bytes 417800 | tf_op jit(solution)/shard_map/ppermute | solution.py:291
  13.1 0.0 copy-done.1
  13.1 0.0 copy-done.2
  13.1 0.0 copy-done
  13.2 0.0 copy-done.3
  13.2 6.4 %local_part.1 = (bf16[16,640,256]{2,1,0:T(8,128)(2,1)S(1)}, bf16[256,2048]{1,0:T(8,128)(2,1)S(1)}, bf16[256,2048]{1,0:T(8,128)(2,1)S(1)}, bf16[3,16,2048]{2,1,0:...) custom-call(bf16[3,256,2048]{2,1,0:T(8,128)(2,1)} %bitcast.17, bf16[256,2048]{1,0:T(8,128)(2,1)S(1)} %copy-done, ...), custom_call_target="tpu_custom_call" | custom-call | flops 1000000000 | bytes 16777216 | tf_op jit(solution)/shard_map/local_part/pallas_call | solution.py:159
  19.6 0.8 %collective-permute-done.2.carry_ref = bf16[136,768]{1,0:T(8,128)(2,1)S(1)} collective-permute-done((bf16[136,768]{1,0:T(8,128)(2,1)S(1)}, bf16[136,768]{1,0:T(8,128)(2,1)S(1)}, u32[]{:S(2)}, u32[]{:S(2)}) %collective-permute-start.2) | collective-permute-done | bytes 208928 | tf_op jit(solution)/shard_map/ppermute | solution.py:291
  20.3 0.8 %head_part.3 = (bf16[160,768]{1,0:T(8,128)(2,1)S(1)}, f32[256,128]{1,0:T(8,128)S(1)}) custom-call(bf16[136,768]{1,0:T(8,128)(2,1)S(1)} %collective-permute-done.2.carry_ref, bf16[3,16,2048]{2,1,0:T(8,128)(2,1)S(1)} %get-tuple-element.17.first_ref, bf16[256,2048]{1,0:T(8,128)(2,1)S(1)} %copy-done, f32[3,3,2048]{2,1,0:T(4,128)S(1)} %copy-done.1, ...), custom_call_target="tpu_custom_call" | custom-call | tf_op jit(solution)/shard_map/head_part/pallas_call | solution.py:224
  21.1 3.7 %collective-permute-done.1.carry_ref = bf16[136,768]{1,0:T(8,128)(2,1)S(1)} collective-permute-done((bf16[136,768]{1,0:T(8,128)(2,1)S(1)}, bf16[136,768]{1,0:T(8,128)(2,1)S(1)}, u32[]{:S(2)}, u32[]{:S(2)}) %collective-permute-start.1) | collective-permute-done | bytes 208928 | tf_op jit(solution)/shard_map/ppermute | solution.py:291
  24.8 0.8 %head_part.4 = (bf16[160,768]{1,0:T(8,128)(2,1)S(1)}, f32[256,128]{1,0:T(8,128)S(1)}) custom-call(bf16[136,768]{1,0:T(8,128)(2,1)S(1)} %collective-permute-done.1.carry_ref, bf16[3,16,2048]{2,1,0:T(8,128)(2,1)S(1)} %get-tuple-element.17.first_ref, bf16[256,2048]{1,0:T(8,128)(2,1)S(1)} %copy-done, f32[3,3,2048]{2,1,0:T(4,128)S(1)} %copy-done.1, ...), custom_call_target="tpu_custom_call" | custom-call | tf_op jit(solution)/shard_map/head_part/pallas_call | solution.py:224
  25.6 0.0 copy-start.4
  25.6 2.2 %collective-permute-done.carry_ref = bf16[136,512]{1,0:T(8,128)(2,1)S(1)} collective-permute-done((bf16[136,512]{1,0:T(8,128)(2,1)S(1)}, bf16[136,512]{1,0:T(8,128)(2,1)S(1)}, u32[]{:S(2)}, u32[]{:S(2)}) %collective-permute-start) | collective-permute-done | bytes 139296 | tf_op jit(solution)/shard_map/ppermute | solution.py:291
  27.8 0.7 %head_part.5 = (bf16[160,512]{1,0:T(8,128)(2,1)S(1)}, f32[8,256]{1,0:T(8,128)S(1)}) custom-call(bf16[136,512]{1,0:T(8,128)(2,1)S(1)} %collective-permute-done.carry_ref, bf16[3,16,2048]{2,1,0:T(8,128)(2,1)S(1)} %get-tuple-element.17.first_ref, bf16[256,2048]{1,0:T(8,128)(2,1)S(1)} %copy-done, f32[3,3,2048]{2,1,0:T(4,128)S(1)} %copy-done.1, ...), custom_call_target="tpu_custom_call" | custom-call | tf_op jit(solution)/shard_map/head_part/pallas_call | solution.py:224
  28.5 6.1 %all-gather = f32[4,1,256]{2,1,0:T(1,128)S(1)} all-gather(f32[1,1,256]{2,1,0:T(1,128)S(1)} %slice_bitcast_fusion), channel_id=1, replica_groups=mesh['ctx'=128,'tp'=4] {'tp'}, dimensions={0}, use_global_device_ids=true | all-gather | bytes 5120 | tf_op jit(solution)/shard_map/all_gather | solution.py:298
  34.6 0.0 copy-done.4
  34.6 1.2 %normalize.1 = bf16[256,2048]{1,0:T(8,128)(2,1)} custom-call(f32[4,256]{1,0:T(4,128)S(1)} %bitcast.12, bf16[160,768]{1,0:T(8,128)(2,1)S(1)} %get-tuple-element.25.refs_0_, bf16[160,768]{1,0:T(8,128)(2,1)S(1)} %get-tuple-element.26.refs_1_, bf16[160,512]{1,0:T(8,128)(2,1)S(1)} %get-tuple-element.27.refs_2_, bf16[96,2048]{1,0:T(8,128)(2,1)S(1)} %get-tuple-element.28.refs_3_, ...), custom_call_target="tpu_custom_call" | custom-call | tf_op jit(solution)/shard_map/normalize/pallas_call | solution.py:271
  (2 shorter events, 0.0 us)
Async XLA Ops:
  0.0 13.1 %copy-start.1 = (f32[3,3,2048]{2,1,0:T(4,128)S(1)}, f32[3,3,2048]{2,1,0:T(4,128)}, u32[]{:S(2)}) copy-start(f32[3,3,2048]{2,1,0:T(4,128)} %short_ref.13) | copy-start | bytes 221188
  0.0 13.1 %copy-start.2 = (f32[2048]{0:T(1024)S(1)}, f32[2048]{0:T(1024)}, u32[]{:S(2)}) copy-start(f32[2048]{0:T(1024)} %param.10) | copy-start | bytes 24580
  0.0 13.1 %copy-start = (bf16[256,2048]{1,0:T(8,128)(2,1)S(1)}, bf16[256,2048]{1,0:T(8,128)(2,1)}, u32[]{:S(2)}) copy-start(bf16[256,2048]{1,0:T(8,128)(2,1)} %res_ref.7) | copy-start | bytes 3145732
  0.0 13.1 %copy-start.3 = (bf16[128,128]{1,0:T(8,128)(2,1)S(1)}, bf16[128,128]{1,0:T(8,128)(2,1)}, u32[]{:S(2)}) copy-start(bf16[128,128]{1,0:T(8,128)(2,1)} %filt_ref.1) | copy-start | bytes 98308
  1.5 18.9 %collective-permute-start.2 = (bf16[136,768]{1,0:T(8,128)(2,1)S(1)}, bf16[136,768]{1,0:T(8,128)(2,1)S(1)}, u32[]{:S(2)}, u32[]{:S(2)}) collective-permute-start(bf16[136,768]{1,0:T(8,128)(2,1)S(1)} %tail_gate.5), channel_id=1, source_target_pairs={{0,4},{4,8},{8,12},{12,16},{16,20},{20,24},{24,28},{28,32},{32,36}... | collective-permute-start | bytes 626696 | tf_op jit(solution)/shard_map/ppermute | solution.py:291
  6.0 18.9 %collective-permute-start.1 = (bf16[136,768]{1,0:T(8,128)(2,1)S(1)}, bf16[136,768]{1,0:T(8,128)(2,1)S(1)}, u32[]{:S(2)}, u32[]{:S(2)}) collective-permute-start(bf16[136,768]{1,0:T(8,128)(2,1)S(1)} %tail_gate.4), channel_id=1, source_target_pairs={{0,4},{4,8},{8,12},{12,16},{16,20},{20,24},{24,28},{28,32},{32,36}... | collective-permute-start | bytes 626696 | tf_op jit(solution)/shard_map/ppermute | solution.py:291
  10.3 17.5 %collective-permute-start = (bf16[136,512]{1,0:T(8,128)(2,1)S(1)}, bf16[136,512]{1,0:T(8,128)(2,1)S(1)}, u32[]{:S(2)}, u32[]{:S(2)}) collective-permute-start(bf16[136,512]{1,0:T(8,128)(2,1)S(1)} %tail_gate.3), channel_id=1, source_target_pairs={{0,4},{4,8},{8,12},{12,16},{16,20},{20,24},{24,28},{28,32},{32,36}... | collective-permute-start | bytes 417800 | tf_op jit(solution)/shard_map/ppermute | solution.py:291
  25.6 9.0 %copy-start.4 = (f32[2048]{0:T(1024)S(1)}, f32[2048]{0:T(1024)}, u32[]{:S(2)}) copy-start(f32[2048]{0:T(1024)} %param.11) | copy-start | bytes 24580

commit v3 on v2

--- a/solution.py
+++ b/solution.py
@@ -13,7 +13,7 @@
 HEAD = 80
 TAIL = 48
 EPS = 1e-06
-WIDTHS = (768, 768, 512)
+WIDTHS = (896, 896, 256)
 UNROLL = 2
 NORM_BLOCKS = 4
 VMEM = pl.BlockSpec(memory_space=pltpu.VMEM)
@@ -63,7 +63,7 @@
 
 
 def tail_gate(feats, short_taps, begin, width):
-    halo = 16
+    halo = 8
     return pl.pallas_call(
         functools.partial(tail_gate_kernel, begin),
         in_specs=[pl.BlockSpec(memory_space=pltpu.HBM)] * 2,
@@ -288,7 +288,10 @@
     route = [(i, i + 1) for i in range(size - 1)]
     starts = [sum(WIDTHS[:i]) for i in range(len(WIDTHS))]
     parts = [tail_gate(feats, short_taps, s, w) for s, w in zip(starts, WIDTHS)]
-    carries = [lax.ppermute(part, "ctx", route) for part in parts]
+    cut = size // 2 - 1
+    early = [pair for pair in route if pair != (cut - 1, cut)]
+    carries = [lax.ppermute(part, "ctx", route if i else early) for i, part in enumerate(parts)]
+    carries[0] = carries[0] + lax.ppermute(parts[0], "ctx", [(cut - 1, cut)])
     toep, gate, query, first, tail, ss = local_part(feats, residual, short_taps, filter_taps, skip)
     heads = []
     for start, carry in zip(starts, carries):

time: 36.1 us -> 35.3 us (0.978)
  waiting for transfers between devices: 6.62 us -> 5.45 us
  starting transfers between devices: 9.06 us -> 9.74 us
    ppermute x3 -> x4, waiting for transfers between devices: 6.62 us -> 5.45 us  [the longest x3 5.45 us: on_device(): lax.ppermute(part, 'ctx', route if i else early)]
    ppermute x3 -> x4, starting transfers between devices: 9.06 us -> 9.74 us  [the longest x3 9.06 us: on_device(): lax.ppermute(part, 'ctx', route if i else early)]
  transfers between devices with their start and end apart: 3 -> 4, of which waited for: 3 -> 3; matrix products, arithmetic and copies ran while one was open for 0% -> 0% of each run, Pallas kernels for 29% -> 30%
where the time goes in v3:
time: 35.3 us; the launch traced here: 35.1 us
  Pallas kernels  13.9 us (39%)
  starting transfers between devices  9.74 us (28%)
  blocking collectives  5.8 us (16%)
  waiting for transfers between devices  5.45 us (15%)
    ppermute x3, starting transfers between devices, on_device(): lax.ppermute(part, 'ctx', route if i else early)  9.06 us
    pallas_call x1, Pallas kernels, local_part(): pl.pallas_call(local_kernel, in_specs=[pl.BlockSpec(memory_space=pltpu.HB...  6.4 us
    all_gather x1, blocking collectives, on_device(): ss = lax.all_gather(ss[0], 'tp')  5.8 us
    ppermute x3, waiting for transfers between devices, on_device(): lax.ppermute(part, 'ctx', route if i else early)  5.45 us
    pallas_call x3, Pallas kernels, tail_gate(): pl.pallas_call(functools.partial(tail_gate_kernel, begin), in_specs=[pl.B...  3.97 us
    pallas_call x3, Pallas kernels, head_part(): pl.pallas_call(functools.partial(head_kernel, start), in_specs=[VMEM] * 9...  2.28 us
    pallas_call x1, Pallas kernels, normalize(): pl.pallas_call(functools.partial(norm_kernel, width), in_specs=[VMEM] * (...  1.23 us
  transfers between devices with their start and end apart: 4, of which 3 were waited for; matrix products, arithmetic and copies ran while one was open for 0% of the time, Pallas kernels for 30%

profile of v3, /device:TPU:25, one launch (start us, length us, event | category | flops | bytes accessed | tf_op | source)
XLA Modules:
  0.0 35.1 jit_solution(17830592396042146905)
XLA Ops:
  0.0 0.0 copy-start.1
  0.0 0.0 copy-start.2
  0.0 0.0 copy-start
  0.0 0.0 copy-start.3
  0.0 1.5 %tail_gate.5 = bf16[136,896]{1,0:T(8,128)(2,1)S(1)} custom-call(bf16[3,256,2048]{2,1,0:T(8,128)(2,1)} %bitcast.14, f32[3,3,2048]{2,1,0:T(4,128)} %short_ref.13), custom_call_target="tpu_custom_call" | custom-call | tf_op jit(solution)/shard_map/tail_gate/pallas_call | solution.py:67
  1.5 3.1 %collective-permute-start.2 = (bf16[136,896]{1,0:T(8,128)(2,1)S(1)}, bf16[136,896]{1,0:T(8,128)(2,1)S(1)}, u32[]{:S(2)}, u32[]{:S(2)}) collective-permute-start(bf16[136,896]{1,0:T(8,128)(2,1)S(1)} %tail_gate.5), channel_id=1, source_target_pairs={{0,4},{4,8},{8,12},{12,16},{16,20},{20,24},{24,28},{28,32},{32,36}... | collective-permute-start | bytes 731144 | tf_op jit(solution)/shard_map/ppermute | solution.py:293
  4.7 0.7 %collective-permute-start.3 = (bf16[136,896]{1,0:T(8,128)(2,1)S(1)}, bf16[136,896]{1,0:T(8,128)(2,1)S(1)}, u32[]{:S(2)}, u32[]{:S(2)}) collective-permute-start(bf16[136,896]{1,0:T(8,128)(2,1)S(1)} %tail_gate.5), channel_id=1, source_target_pairs={{248,252},{249,253},{250,254},{251,255}} | collective-permute-start | bytes 731144 | tf_op jit(solution)/shard_map/ppermute | solution.py:294
  5.3 1.4 %tail_gate.4 = bf16[136,896]{1,0:T(8,128)(2,1)S(1)} custom-call(bf16[3,256,2048]{2,1,0:T(8,128)(2,1)} %bitcast.15, f32[3,3,2048]{2,1,0:T(4,128)} %short_ref.13), custom_call_target="tpu_custom_call" | custom-call | tf_op jit(solution)/shard_map/tail_gate/pallas_call | solution.py:67
  6.8 3.1 %collective-permute-start.1 = (bf16[136,896]{1,0:T(8,128)(2,1)S(1)}, bf16[136,896]{1,0:T(8,128)(2,1)S(1)}, u32[]{:S(2)}, u32[]{:S(2)}) collective-permute-start(bf16[136,896]{1,0:T(8,128)(2,1)S(1)} %tail_gate.4), channel_id=1, source_target_pairs={{0,4},{4,8},{8,12},{12,16},{16,20},{20,24},{24,28},{28,32},{32,36}... | collective-permute-start | bytes 731144 | tf_op jit(solution)/shard_map/ppermute | solution.py:293
  9.9 1.1 %tail_gate.3 = bf16[136,256]{1,0:T(8,128)(2,1)S(1)} custom-call(bf16[3,256,2048]{2,1,0:T(8,128)(2,1)} %bitcast.16, f32[3,3,2048]{2,1,0:T(4,128)} %short_ref.13), custom_call_target="tpu_custom_call" | custom-call | tf_op jit(solution)/shard_map/tail_gate/pallas_call | solution.py:67
  10.9 2.8 %collective-permute-start = (bf16[136,256]{1,0:T(8,128)(2,1)S(1)}, bf16[136,256]{1,0:T(8,128)(2,1)S(1)}, u32[]{:S(2)}, u32[]{:S(2)}) collective-permute-start(bf16[136,256]{1,0:T(8,128)(2,1)S(1)} %tail_gate.3), channel_id=1, source_target_pairs={{0,4},{4,8},{8,12},{12,16},{16,20},{20,24},{24,28},{28,32},{32,36}... | collective-permute-start | bytes 208904 | tf_op jit(solution)/shard_map/ppermute | solution.py:293
  13.8 0.0 copy-done.1
  13.8 0.0 copy-done.2
  13.8 0.0 copy-done
  13.8 0.0 copy-done.3
  13.8 6.4 %local_part.1 = (bf16[16,640,256]{2,1,0:T(8,128)(2,1)S(1)}, bf16[256,2048]{1,0:T(8,128)(2,1)S(1)}, bf16[256,2048]{1,0:T(8,128)(2,1)S(1)}, bf16[3,16,2048]{2,1,0:...) custom-call(bf16[3,256,2048]{2,1,0:T(8,128)(2,1)} %bitcast.17, bf16[256,2048]{1,0:T(8,128)(2,1)S(1)} %copy-done, ...), custom_call_target="tpu_custom_call" | custom-call | flops 1000000000 | bytes 16777216 | tf_op jit(solution)/shard_map/local_part/pallas_call | solution.py:159
  20.2 0.3 collective-permute-done.2
  20.5 0.0 collective-permute-done.3
  20.5 0.1 add.3.carry_ref
  20.6 0.9 %head_part.3 = (bf16[160,896]{1,0:T(8,128)(2,1)S(1)}, f32[256,128]{1,0:T(8,128)S(1)}) custom-call(bf16[136,896]{1,0:T(8,128)(2,1)S(1)} %add.3.carry_ref, bf16[3,16,2048]{2,1,0:T(8,128)(2,1)S(1)} %get-tuple-element.17.first_ref, bf16[256,2048]{1,0:T(8,128)(2,1)S(1)} %copy-done, f32[3,3,2048]{2,1,0:T(4,128)S(1)} %copy-done.1, f32[1,2048]{1,0:T(1,128)S(1)} %bitcast.9, ...), custom_call_target="tpu_custom_call" | custom-call | tf_op jit(solution)/shard_map/head_part/pallas_call | solution.py:224
  21.5 4.6 %collective-permute-done.1.carry_ref = bf16[136,896]{1,0:T(8,128)(2,1)S(1)} collective-permute-done((bf16[136,896]{1,0:T(8,128)(2,1)S(1)}, bf16[136,896]{1,0:T(8,128)(2,1)S(1)}, u32[]{:S(2)}, u32[]{:S(2)}) %collective-permute-start.1) | collective-permute-done | bytes 243744 | tf_op jit(solution)/shard_map/ppermute | solution.py:293
  26.1 0.9 %head_part.4 = (bf16[160,896]{1,0:T(8,128)(2,1)S(1)}, f32[256,128]{1,0:T(8,128)S(1)}) custom-call(bf16[136,896]{1,0:T(8,128)(2,1)S(1)} %collective-permute-done.1.carry_ref, bf16[3,16,2048]{2,1,0:T(8,128)(2,1)S(1)} %get-tuple-element.17.first_ref, bf16[256,2048]{1,0:T(8,128)(2,1)S(1)} %copy-done, f32[3,3,2048]{2,1,0:T(4,128)S(1)} %copy-done.1, ...), custom_call_target="tpu_custom_call" | custom-call | tf_op jit(solution)/shard_map/head_part/pallas_call | solution.py:224
  27.0 0.0 copy-start.4
  27.0 0.6 %collective-permute-done.carry_ref = bf16[136,256]{1,0:T(8,128)(2,1)S(1)} collective-permute-done((bf16[136,256]{1,0:T(8,128)(2,1)S(1)}, bf16[136,256]{1,0:T(8,128)(2,1)S(1)}, u32[]{:S(2)}, u32[]{:S(2)}) %collective-permute-start) | collective-permute-done | bytes 69664 | tf_op jit(solution)/shard_map/ppermute | solution.py:293
  27.6 0.5 %head_part.5 = (bf16[160,256]{1,0:T(8,128)(2,1)S(1)}, f32[8,256]{1,0:T(8,128)S(1)}) custom-call(bf16[136,256]{1,0:T(8,128)(2,1)S(1)} %collective-permute-done.carry_ref, bf16[3,16,2048]{2,1,0:T(8,128)(2,1)S(1)} %get-tuple-element.17.first_ref, bf16[256,2048]{1,0:T(8,128)(2,1)S(1)} %copy-done, f32[3,3,2048]{2,1,0:T(4,128)S(1)} %copy-done.1, ...), custom_call_target="tpu_custom_call" | custom-call | tf_op jit(solution)/shard_map/head_part/pallas_call | solution.py:224
  28.1 5.8 %all-gather = f32[4,1,256]{2,1,0:T(1,128)S(1)} all-gather(f32[1,1,256]{2,1,0:T(1,128)S(1)} %slice_bitcast_fusion), channel_id=1, replica_groups=mesh['ctx'=128,'tp'=4] {'tp'}, dimensions={0}, use_global_device_ids=true | all-gather | bytes 5120 | tf_op jit(solution)/shard_map/all_gather | solution.py:301
  33.9 0.0 copy-done.4
  33.9 1.2 %normalize.1 = bf16[256,2048]{1,0:T(8,128)(2,1)} custom-call(f32[4,256]{1,0:T(4,128)S(1)} %bitcast.12, bf16[160,896]{1,0:T(8,128)(2,1)S(1)} %get-tuple-element.25.refs_0_, bf16[160,896]{1,0:T(8,128)(2,1)S(1)} %get-tuple-element.26.refs_1_, bf16[160,256]{1,0:T(8,128)(2,1)S(1)} %get-tuple-element.27.refs_2_, bf16[96,2048]{1,0:T(8,128)(2,1)S(1)} %get-tuple-element.28.refs_3_, ...), custom_call_target="tpu_custom_call" | custom-call | tf_op jit(solution)/shard_map/normalize/pallas_call | solution.py:271
  (2 shorter events, 0.0 us)
Async XLA Ops:
  0.0 13.8 %copy-start.1 = (f32[3,3,2048]{2,1,0:T(4,128)S(1)}, f32[3,3,2048]{2,1,0:T(4,128)}, u32[]{:S(2)}) copy-start(f32[3,3,2048]{2,1,0:T(4,128)} %short_ref.13) | copy-start | bytes 221188
  0.0 13.8 %copy-start.2 = (f32[2048]{0:T(1024)S(1)}, f32[2048]{0:T(1024)}, u32[]{:S(2)}) copy-start(f32[2048]{0:T(1024)} %param.10) | copy-start | bytes 24580
  0.0 13.8 %copy-start = (bf16[256,2048]{1,0:T(8,128)(2,1)S(1)}, bf16[256,2048]{1,0:T(8,128)(2,1)}, u32[]{:S(2)}) copy-start(bf16[256,2048]{1,0:T(8,128)(2,1)} %res_ref.7) | copy-start | bytes 3145732
  0.0 13.8 %copy-start.3 = (bf16[128,128]{1,0:T(8,128)(2,1)S(1)}, bf16[128,128]{1,0:T(8,128)(2,1)}, u32[]{:S(2)}) copy-start(bf16[128,128]{1,0:T(8,128)(2,1)} %filt_ref.1) | copy-start | bytes 98308
  1.5 19.0 %collective-permute-start.2 = (bf16[136,896]{1,0:T(8,128)(2,1)S(1)}, bf16[136,896]{1,0:T(8,128)(2,1)S(1)}, u32[]{:S(2)}, u32[]{:S(2)}) collective-permute-start(bf16[136,896]{1,0:T(8,128)(2,1)S(1)} %tail_gate.5), channel_id=1, source_target_pairs={{0,4},{4,8},{8,12},{12,16},{16,20},{20,24},{24,28},{28,32},{32,36}... | collective-permute-start | bytes 731144 | tf_op jit(solution)/shard_map/ppermute | solution.py:293
  4.7 15.9 %collective-permute-start.3 = (bf16[136,896]{1,0:T(8,128)(2,1)S(1)}, bf16[136,896]{1,0:T(8,128)(2,1)S(1)}, u32[]{:S(2)}, u32[]{:S(2)}) collective-permute-start(bf16[136,896]{1,0:T(8,128)(2,1)S(1)} %tail_gate.5), channel_id=1, source_target_pairs={{248,252},{249,253},{250,254},{251,255}} | collective-permute-start | bytes 731144 | tf_op jit(solution)/shard_map/ppermute | solution.py:294
  6.8 19.3 %collective-permute-start.1 = (bf16[136,896]{1,0:T(8,128)(2,1)S(1)}, bf16[136,896]{1,0:T(8,128)(2,1)S(1)}, u32[]{:S(2)}, u32[]{:S(2)}) collective-permute-start(bf16[136,896]{1,0:T(8,128)(2,1)S(1)} %tail_gate.4), channel_id=1, source_target_pairs={{0,4},{4,8},{8,12},{12,16},{16,20},{20,24},{24,28},{28,32},{32,36}... | collective-permute-start | bytes 731144 | tf_op jit(solution)/shard_map/ppermute | solution.py:293
  10.9 16.6 %collective-permute-start = (bf16[136,256]{1,0:T(8,128)(2,1)S(1)}, bf16[136,256]{1,0:T(8,128)(2,1)S(1)}, u32[]{:S(2)}, u32[]{:S(2)}) collective-permute-start(bf16[136,256]{1,0:T(8,128)(2,1)S(1)} %tail_gate.3), channel_id=1, source_target_pairs={{0,4},{4,8},{8,12},{12,16},{16,20},{20,24},{24,28},{28,32},{32,36}... | collective-permute-start | bytes 208904 | tf_op jit(solution)/shard_map/ppermute | solution.py:293
  27.0 6.9 %copy-start.4 = (f32[2048]{0:T(1024)S(1)}, f32[2048]{0:T(1024)}, u32[]{:S(2)}) copy-start(f32[2048]{0:T(1024)} %param.11) | copy-start | bytes 24580

commit v4 on v3

--- a/solution.py
+++ b/solution.py
@@ -15,13 +15,17 @@
 EPS = 1e-06
 WIDTHS = (896, 896, 256)
 UNROLL = 2
-NORM_BLOCKS = 4
+NORM_BLOCKS = 8
 VMEM = pl.BlockSpec(memory_space=pltpu.VMEM)
 MIB = 1 << 20
 
 
 def in_hbm(x):
     return pltpu.with_memory_space_constraint(x, pltpu.HBM)
+
+
+def rounded(x):
+    return x.astype(BF16).astype(F32)
 
 
 def causal3(x, w):
@@ -31,7 +35,7 @@
 def gate_tile(load_kv, last_q, taps, halo):
     raw = [load_kv(s).astype(F32) for s in range(2)]
     feat = [causal3(raw[s], taps[s])[halo:] for s in range(2)]
-    gate = (feat[0] * feat[1]).astype(BF16)
+    gate = (rounded(feat[0]) * rounded(feat[1])).astype(BF16)
     last_q = pltpu.roll(last_q.astype(F32)[-8:], 2, 0)
     last_k = pltpu.roll(raw[0][-8:], 4, 0)
     last_v = pltpu.roll(raw[1][-8:], 6, 0)
@@ -115,9 +119,10 @@
             causal3(feats_ref[s, :, lanes].astype(F32), [short_ref[i, s : s + 1, lanes] for i in range(3)])
             for s in range(3)
         ]
-        gate = (feats[1] * feats[2]).astype(BF16)
+        gate = (rounded(feats[1]) * rounded(feats[2])).astype(BF16)
+        query = feats[0].astype(BF16)
         gate_ref[:, lanes] = gate
-        q_ref[:, lanes] = feats[0].astype(BF16)
+        q_ref[:, lanes] = query
         taps = filt_ref[pl.ds(pl.multiple_of(t * per_tile, per_tile), per_tile), :]
         base = jnp.dot(taps, flip, preferred_element_type=F32)
         lhs = []
@@ -138,7 +143,7 @@
         prod = jnp.dot(jnp.concatenate(lhs, 0), rhs, preferred_element_type=F32)
         filtered = group_select(prod, per_tile, TAIL)
         filtered = filtered + skip_ref[:, lanes] * gate[first:].astype(F32)
-        stream = (res_ref[first:, lanes].astype(F32) + feats[0][first:] * filtered).astype(BF16)
+        stream = (res_ref[first:, lanes].astype(F32) + query[first:].astype(F32) * filtered).astype(BF16)
         stream_ref[:, lanes] = stream
         wide_stream = stream.astype(F32)
         return wide_stream * wide_stream
@@ -196,7 +201,7 @@
             x1 = jnp.where(row == 0, newer, pltpu.roll(x, 1, 0))
             x2 = jnp.where(row == 0, older, jnp.where(row == 1, newer, pltpu.roll(x, 2, 0)))
             feats.append(w[0] * x + w[1] * x1 + w[2] * x2)
-        fixed = (feats[1] * feats[2]).astype(BF16)
+        fixed = (rounded(feats[1]) * rounded(feats[2])).astype(BF16)
         gate = jnp.concatenate([fixed, gate_ref[16 : LANES + HEAD, lanes]], 0)
         query = jnp.concatenate([feats[0].astype(BF16), q_ref[16:rows, lanes]], 0)
         rhs = jnp.concatenate(

time: 35.3 us -> 35.3 us (level)
  Pallas kernels: 13.9 us -> 14.3 us
  waiting for transfers between devices: 5.45 us -> 5.08 us
    ppermute x3, waiting for transfers between devices: 5.45 us -> 5.08 us  [on_device(): lax.ppermute(part, 'ctx', route if i else early)]
  transfers between devices with their start and end apart: 4 -> 4, of which waited for: 3 -> 2; matrix products, arithmetic and copies ran while one was open for 0% -> 0% of each run, Pallas kernels for 30% -> 31%
where the time goes in v4:
time: 35.3 us; the launch traced here: 35.1 us
  Pallas kernels  14.3 us (41%)
  starting transfers between devices  9.74 us (28%)
  blocking collectives  5.74 us (16%)
  waiting for transfers between devices  5.08 us (14%)
    ppermute x3, starting transfers between devices, on_device(): lax.ppermute(part, 'ctx', route if i else early)  9.06 us
    pallas_call x1, Pallas kernels, local_part(): pl.pallas_call(local_kernel, in_specs=[pl.BlockSpec(memory_space=pltpu.HB...  6.72 us
    all_gather x1, blocking collectives, on_device(): ss = lax.all_gather(ss[0], 'tp')  5.74 us
    ppermute x3, waiting for transfers between devices, on_device(): lax.ppermute(part, 'ctx', route if i else early)  5.08 us
    pallas_call x3, Pallas kernels, tail_gate(): pl.pallas_call(functools.partial(tail_gate_kernel, begin), in_specs=[pl.B...  4.07 us
    pallas_call x3, Pallas kernels, head_part(): pl.pallas_call(functools.partial(head_kernel, start), in_specs=[VMEM] * 9...  2.29 us
    pallas_call x1, Pallas kernels, normalize(): pl.pallas_call(functools.partial(norm_kernel, width), in_specs=[VMEM] * (...  1.21 us
  transfers between devices with their start and end apart: 4, of which 2 were waited for; matrix products, arithmetic and copies ran while one was open for 0% of the time, Pallas kernels for 31%

profile of v4, /device:TPU:25, one launch (start us, length us, event | category | flops | bytes accessed | tf_op | source)
XLA Modules:
  0.0 35.1 jit_solution(4447154371838081977)
XLA Ops:
  0.0 0.0 copy-start.1
  0.0 0.0 copy-start.2
  0.0 0.0 copy-start
  0.0 0.0 copy-start.3
  0.0 1.5 %tail_gate.5 = bf16[136,896]{1,0:T(8,128)(2,1)S(1)} custom-call(bf16[3,256,2048]{2,1,0:T(8,128)(2,1)} %bitcast.14, f32[3,3,2048]{2,1,0:T(4,128)} %short_ref.13), custom_call_target="tpu_custom_call" | custom-call | tf_op jit(solution)/shard_map/tail_gate/pallas_call | solution.py:71
  1.6 3.1 %collective-permute-start.2 = (bf16[136,896]{1,0:T(8,128)(2,1)S(1)}, bf16[136,896]{1,0:T(8,128)(2,1)S(1)}, u32[]{:S(2)}, u32[]{:S(2)}) collective-permute-start(bf16[136,896]{1,0:T(8,128)(2,1)S(1)} %tail_gate.5), channel_id=1, source_target_pairs={{0,4},{4,8},{8,12},{12,16},{16,20},{20,24},{24,28},{28,32},{32,36}... | collective-permute-start | bytes 731144 | tf_op jit(solution)/shard_map/ppermute | solution.py:298
  4.7 0.7 %collective-permute-start.3 = (bf16[136,896]{1,0:T(8,128)(2,1)S(1)}, bf16[136,896]{1,0:T(8,128)(2,1)S(1)}, u32[]{:S(2)}, u32[]{:S(2)}) collective-permute-start(bf16[136,896]{1,0:T(8,128)(2,1)S(1)} %tail_gate.5), channel_id=1, source_target_pairs={{248,252},{249,253},{250,254},{251,255}} | collective-permute-start | bytes 731144 | tf_op jit(solution)/shard_map/ppermute | solution.py:299
  5.4 1.5 %tail_gate.4 = bf16[136,896]{1,0:T(8,128)(2,1)S(1)} custom-call(bf16[3,256,2048]{2,1,0:T(8,128)(2,1)} %bitcast.15, f32[3,3,2048]{2,1,0:T(4,128)} %short_ref.13), custom_call_target="tpu_custom_call" | custom-call | tf_op jit(solution)/shard_map/tail_gate/pallas_call | solution.py:71
  6.9 3.1 %collective-permute-start.1 = (bf16[136,896]{1,0:T(8,128)(2,1)S(1)}, bf16[136,896]{1,0:T(8,128)(2,1)S(1)}, u32[]{:S(2)}, u32[]{:S(2)}) collective-permute-start(bf16[136,896]{1,0:T(8,128)(2,1)S(1)} %tail_gate.4), channel_id=1, source_target_pairs={{0,4},{4,8},{8,12},{12,16},{16,20},{20,24},{24,28},{28,32},{32,36}... | collective-permute-start | bytes 731144 | tf_op jit(solution)/shard_map/ppermute | solution.py:298
  10.0 1.1 %tail_gate.3 = bf16[136,256]{1,0:T(8,128)(2,1)S(1)} custom-call(bf16[3,256,2048]{2,1,0:T(8,128)(2,1)} %bitcast.16, f32[3,3,2048]{2,1,0:T(4,128)} %short_ref.13), custom_call_target="tpu_custom_call" | custom-call | tf_op jit(solution)/shard_map/tail_gate/pallas_call | solution.py:71
  11.1 2.8 %collective-permute-start = (bf16[136,256]{1,0:T(8,128)(2,1)S(1)}, bf16[136,256]{1,0:T(8,128)(2,1)S(1)}, u32[]{:S(2)}, u32[]{:S(2)}) collective-permute-start(bf16[136,256]{1,0:T(8,128)(2,1)S(1)} %tail_gate.3), channel_id=1, source_target_pairs={{0,4},{4,8},{8,12},{12,16},{16,20},{20,24},{24,28},{28,32},{32,36}... | collective-permute-start | bytes 208904 | tf_op jit(solution)/shard_map/ppermute | solution.py:298
  13.9 0.0 copy-done.1
  13.9 0.0 copy-done.2
  13.9 0.0 copy-done
  13.9 0.0 copy-done.3
  13.9 6.7 %local_part.1 = (bf16[16,640,256]{2,1,0:T(8,128)(2,1)S(1)}, bf16[256,2048]{1,0:T(8,128)(2,1)S(1)}, bf16[256,2048]{1,0:T(8,128)(2,1)S(1)}, bf16[3,16,2048]{2,1,0:...) custom-call(bf16[3,256,2048]{2,1,0:T(8,128)(2,1)} %bitcast.17, bf16[256,2048]{1,0:T(8,128)(2,1)S(1)} %copy-done, ...), custom_call_target="tpu_custom_call" | custom-call | flops 1000000000 | bytes 16777216 | tf_op jit(solution)/shard_map/local_part/pallas_call | solution.py:164
  20.7 0.0 collective-permute-done.2
  20.7 0.0 collective-permute-done.3
  20.7 0.1 add.3.carry_ref
  20.7 0.9 %head_part.3 = (bf16[160,896]{1,0:T(8,128)(2,1)S(1)}, f32[256,128]{1,0:T(8,128)S(1)}) custom-call(bf16[136,896]{1,0:T(8,128)(2,1)S(1)} %add.3.carry_ref, bf16[3,16,2048]{2,1,0:T(8,128)(2,1)S(1)} %get-tuple-element.17.first_ref, bf16[256,2048]{1,0:T(8,128)(2,1)S(1)} %copy-done, f32[3,3,2048]{2,1,0:T(4,128)S(1)} %copy-done.1, f32[1,2048]{1,0:T(1,128)S(1)} %bitcast.9, ...), custom_call_target="tpu_custom_call" | custom-call | tf_op jit(solution)/shard_map/head_part/pallas_call | solution.py:229
  21.7 4.5 %collective-permute-done.1.carry_ref = bf16[136,896]{1,0:T(8,128)(2,1)S(1)} collective-permute-done((bf16[136,896]{1,0:T(8,128)(2,1)S(1)}, bf16[136,896]{1,0:T(8,128)(2,1)S(1)}, u32[]{:S(2)}, u32[]{:S(2)}) %collective-permute-start.1) | collective-permute-done | bytes 243744 | tf_op jit(solution)/shard_map/ppermute | solution.py:298
  26.2 0.9 %head_part.4 = (bf16[160,896]{1,0:T(8,128)(2,1)S(1)}, f32[256,128]{1,0:T(8,128)S(1)}) custom-call(bf16[136,896]{1,0:T(8,128)(2,1)S(1)} %collective-permute-done.1.carry_ref, bf16[3,16,2048]{2,1,0:T(8,128)(2,1)S(1)} %get-tuple-element.17.first_ref, bf16[256,2048]{1,0:T(8,128)(2,1)S(1)} %copy-done, f32[3,3,2048]{2,1,0:T(4,128)S(1)} %copy-done.1, ...), custom_call_target="tpu_custom_call" | custom-call | tf_op jit(solution)/shard_map/head_part/pallas_call | solution.py:229
  27.1 0.0 copy-start.4
  27.1 0.6 %collective-permute-done.carry_ref = bf16[136,256]{1,0:T(8,128)(2,1)S(1)} collective-permute-done((bf16[136,256]{1,0:T(8,128)(2,1)S(1)}, bf16[136,256]{1,0:T(8,128)(2,1)S(1)}, u32[]{:S(2)}, u32[]{:S(2)}) %collective-permute-start) | collective-permute-done | bytes 69664 | tf_op jit(solution)/shard_map/ppermute | solution.py:298
  27.7 0.5 %head_part.5 = (bf16[160,256]{1,0:T(8,128)(2,1)S(1)}, f32[8,256]{1,0:T(8,128)S(1)}) custom-call(bf16[136,256]{1,0:T(8,128)(2,1)S(1)} %collective-permute-done.carry_ref, bf16[3,16,2048]{2,1,0:T(8,128)(2,1)S(1)} %get-tuple-element.17.first_ref, bf16[256,2048]{1,0:T(8,128)(2,1)S(1)} %copy-done, f32[3,3,2048]{2,1,0:T(4,128)S(1)} %copy-done.1, ...), custom_call_target="tpu_custom_call" | custom-call | tf_op jit(solution)/shard_map/head_part/pallas_call | solution.py:229
  28.2 5.7 %all-gather = f32[4,1,256]{2,1,0:T(1,128)S(1)} all-gather(f32[1,1,256]{2,1,0:T(1,128)S(1)} %slice_bitcast_fusion), channel_id=1, replica_groups=mesh['ctx'=128,'tp'=4] {'tp'}, dimensions={0}, use_global_device_ids=true | all-gather | bytes 5120 | tf_op jit(solution)/shard_map/all_gather | solution.py:306
  33.9 0.0 copy-done.4
  33.9 1.2 %normalize.1 = bf16[256,2048]{1,0:T(8,128)(2,1)} custom-call(f32[4,256]{1,0:T(4,128)S(1)} %bitcast.12, bf16[160,896]{1,0:T(8,128)(2,1)S(1)} %get-tuple-element.25.refs_0_, bf16[160,896]{1,0:T(8,128)(2,1)S(1)} %get-tuple-element.26.refs_1_, bf16[160,256]{1,0:T(8,128)(2,1)S(1)} %get-tuple-element.27.refs_2_, bf16[96,2048]{1,0:T(8,128)(2,1)S(1)} %get-tuple-element.28.refs_3_, ...), custom_call_target="tpu_custom_call" | custom-call | tf_op jit(solution)/shard_map/normalize/pallas_call | solution.py:276
  (2 shorter events, 0.0 us)
Async XLA Ops:
  0.0 13.9 %copy-start.1 = (f32[3,3,2048]{2,1,0:T(4,128)S(1)}, f32[3,3,2048]{2,1,0:T(4,128)}, u32[]{:S(2)}) copy-start(f32[3,3,2048]{2,1,0:T(4,128)} %short_ref.13) | copy-start | bytes 221188
  0.0 13.9 %copy-start.2 = (f32[2048]{0:T(1024)S(1)}, f32[2048]{0:T(1024)}, u32[]{:S(2)}) copy-start(f32[2048]{0:T(1024)} %param.10) | copy-start | bytes 24580
  0.0 13.9 %copy-start = (bf16[256,2048]{1,0:T(8,128)(2,1)S(1)}, bf16[256,2048]{1,0:T(8,128)(2,1)}, u32[]{:S(2)}) copy-start(bf16[256,2048]{1,0:T(8,128)(2,1)} %res_ref.7) | copy-start | bytes 3145732
  0.0 13.9 %copy-start.3 = (bf16[128,128]{1,0:T(8,128)(2,1)S(1)}, bf16[128,128]{1,0:T(8,128)(2,1)}, u32[]{:S(2)}) copy-start(bf16[128,128]{1,0:T(8,128)(2,1)} %filt_ref.1) | copy-start | bytes 98308
  1.6 19.1 %collective-permute-start.2 = (bf16[136,896]{1,0:T(8,128)(2,1)S(1)}, bf16[136,896]{1,0:T(8,128)(2,1)S(1)}, u32[]{:S(2)}, u32[]{:S(2)}) collective-permute-start(bf16[136,896]{1,0:T(8,128)(2,1)S(1)} %tail_gate.5), channel_id=1, source_target_pairs={{0,4},{4,8},{8,12},{12,16},{16,20},{20,24},{24,28},{28,32},{32,36}... | collective-permute-start | bytes 731144 | tf_op jit(solution)/shard_map/ppermute | solution.py:298
  4.7 16.0 %collective-permute-start.3 = (bf16[136,896]{1,0:T(8,128)(2,1)S(1)}, bf16[136,896]{1,0:T(8,128)(2,1)S(1)}, u32[]{:S(2)}, u32[]{:S(2)}) collective-permute-start(bf16[136,896]{1,0:T(8,128)(2,1)S(1)} %tail_gate.5), channel_id=1, source_target_pairs={{248,252},{249,253},{250,254},{251,255}} | collective-permute-start | bytes 731144 | tf_op jit(solution)/shard_map/ppermute | solution.py:299
  6.9 19.3 %collective-permute-start.1 = (bf16[136,896]{1,0:T(8,128)(2,1)S(1)}, bf16[136,896]{1,0:T(8,128)(2,1)S(1)}, u32[]{:S(2)}, u32[]{:S(2)}) collective-permute-start(bf16[136,896]{1,0:T(8,128)(2,1)S(1)} %tail_gate.4), channel_id=1, source_target_pairs={{0,4},{4,8},{8,12},{12,16},{16,20},{20,24},{24,28},{28,32},{32,36}... | collective-permute-start | bytes 731144 | tf_op jit(solution)/shard_map/ppermute | solution.py:298
  11.1 16.6 %collective-permute-start = (bf16[136,256]{1,0:T(8,128)(2,1)S(1)}, bf16[136,256]{1,0:T(8,128)(2,1)S(1)}, u32[]{:S(2)}, u32[]{:S(2)}) collective-permute-start(bf16[136,256]{1,0:T(8,128)(2,1)S(1)} %tail_gate.3), channel_id=1, source_target_pairs={{0,4},{4,8},{8,12},{12,16},{16,20},{20,24},{24,28},{28,32},{32,36}... | collective-permute-start | bytes 208904 | tf_op jit(solution)/shard_map/ppermute | solution.py:298
  27.1 6.8 %copy-start.4 = (f32[2048]{0:T(1024)S(1)}, f32[2048]{0:T(1024)}, u32[]{:S(2)}) copy-start(f32[2048]{0:T(1024)} %param.11) | copy-start | bytes 24580

commit v5 on v4

--- a/solution.py
+++ b/solution.py
@@ -13,7 +13,7 @@
 HEAD = 80
 TAIL = 48
 EPS = 1e-06
-WIDTHS = (896, 896, 256)
+WIDTHS = (1152, 640, 256)
 UNROLL = 2
 NORM_BLOCKS = 8
 VMEM = pl.BlockSpec(memory_space=pltpu.VMEM)

time: 35.3 us -> 35.5 us (level)
  blocking collectives: 5.74 us -> 6.13 us
    all_gather x1, blocking collectives: 5.74 us -> 6.13 us  [on_device(): ss = lax.all_gather(ss[0], 'tp')]
  transfers between devices with their start and end apart: 4 -> 4, of which waited for: 2 -> 3; matrix products, arithmetic and copies ran while one was open for 0% -> 0% of each run, Pallas kernels for 31% -> 31%
where the time goes in v5:
time: 35.5 us; the launch traced here: 35.3 us
  Pallas kernels  14.3 us (40%)
  starting transfers between devices  9.75 us (27%)
  blocking collectives  6.13 us (17%)
  waiting for transfers between devices  4.86 us (14%)
    ppermute x3, starting transfers between devices, on_device(): lax.ppermute(part, 'ctx', route if i else early)  9.06 us
    pallas_call x1, Pallas kernels, local_part(): pl.pallas_call(local_kernel, in_specs=[pl.BlockSpec(memory_space=pltpu.HB...  6.72 us
    all_gather x1, blocking collectives, on_device(): ss = lax.all_gather(ss[0], 'tp')  6.13 us
    ppermute x3, waiting for transfers between devices, on_device(): lax.ppermute(part, 'ctx', route if i else early)  4.86 us
    pallas_call x3, Pallas kernels, tail_gate(): pl.pallas_call(functools.partial(tail_gate_kernel, begin), in_specs=[pl.B...  4.07 us
    pallas_call x3, Pallas kernels, head_part(): pl.pallas_call(functools.partial(head_kernel, start), in_specs=[VMEM] * 9...  2.28 us
    pallas_call x1, Pallas kernels, normalize(): pl.pallas_call(functools.partial(norm_kernel, width), in_specs=[VMEM] * (...  1.21 us
  transfers between devices with their start and end apart: 4, of which 3 were waited for; matrix products, arithmetic and copies ran while one was open for 0% of the time, Pallas kernels for 31%

profile of v5, /device:TPU:25, one launch (start us, length us, event | category | flops | bytes accessed | tf_op | source)
XLA Modules:
  0.0 35.3 jit_solution(1758143116789988577)
XLA Ops:
  0.0 0.0 copy-start.1
  0.0 0.0 copy-start.2
  0.0 0.0 copy-start
  0.0 0.0 copy-start.3
  0.0 1.7 %tail_gate.5 = bf16[136,1152]{1,0:T(8,128)(2,1)S(1)} custom-call(bf16[3,256,2048]{2,1,0:T(8,128)(2,1)} %bitcast.14, f32[3,3,2048]{2,1,0:T(4,128)} %short_ref.13), custom_call_target="tpu_custom_call" | custom-call | tf_op jit(solution)/shard_map/tail_gate/pallas_call | solution.py:71
  1.7 3.1 %collective-permute-start.2 = (bf16[136,1152]{1,0:T(8,128)(2,1)S(1)}, bf16[136,1152]{1,0:T(8,128)(2,1)S(1)}, u32[]{:S(2)}, u32[]{:S(2)}) collective-permute-start(bf16[136,1152]{1,0:T(8,128)(2,1)S(1)} %tail_gate.5), channel_id=1, source_target_pairs={{0,4},{4,8},{8,12},{12,16},{16,20},{20,24},{24,28},{28,32},{32,36}... | collective-permute-start | bytes 940040 | tf_op jit(solution)/shard_map/ppermute | solution.py:298
  4.9 0.7 %collective-permute-start.3 = (bf16[136,1152]{1,0:T(8,128)(2,1)S(1)}, bf16[136,1152]{1,0:T(8,128)(2,1)S(1)}, u32[]{:S(2)}, u32[]{:S(2)}) collective-permute-start(bf16[136,1152]{1,0:T(8,128)(2,1)S(1)} %tail_gate.5), channel_id=1, source_target_pairs={{248,252},{249,253},{250,254},{251,255}} | collective-permute-start | bytes 940040 | tf_op jit(solution)/shard_map/ppermute | solution.py:299
  5.6 1.3 %tail_gate.4 = bf16[136,640]{1,0:T(8,128)(2,1)S(1)} custom-call(bf16[3,256,2048]{2,1,0:T(8,128)(2,1)} %bitcast.15, f32[3,3,2048]{2,1,0:T(4,128)} %short_ref.13), custom_call_target="tpu_custom_call" | custom-call | tf_op jit(solution)/shard_map/tail_gate/pallas_call | solution.py:71
  6.9 3.1 %collective-permute-start.1 = (bf16[136,640]{1,0:T(8,128)(2,1)S(1)}, bf16[136,640]{1,0:T(8,128)(2,1)S(1)}, u32[]{:S(2)}, u32[]{:S(2)}) collective-permute-start(bf16[136,640]{1,0:T(8,128)(2,1)S(1)} %tail_gate.4), channel_id=1, source_target_pairs={{0,4},{4,8},{8,12},{12,16},{16,20},{20,24},{24,28},{28,32},{32,36}... | collective-permute-start | bytes 522248 | tf_op jit(solution)/shard_map/ppermute | solution.py:298
  10.0 1.1 %tail_gate.3 = bf16[136,256]{1,0:T(8,128)(2,1)S(1)} custom-call(bf16[3,256,2048]{2,1,0:T(8,128)(2,1)} %bitcast.16, f32[3,3,2048]{2,1,0:T(4,128)} %short_ref.13), custom_call_target="tpu_custom_call" | custom-call | tf_op jit(solution)/shard_map/tail_gate/pallas_call | solution.py:71
  11.1 2.8 %collective-permute-start = (bf16[136,256]{1,0:T(8,128)(2,1)S(1)}, bf16[136,256]{1,0:T(8,128)(2,1)S(1)}, u32[]{:S(2)}, u32[]{:S(2)}) collective-permute-start(bf16[136,256]{1,0:T(8,128)(2,1)S(1)} %tail_gate.3), channel_id=1, source_target_pairs={{0,4},{4,8},{8,12},{12,16},{16,20},{20,24},{24,28},{28,32},{32,36}... | collective-permute-start | bytes 208904 | tf_op jit(solution)/shard_map/ppermute | solution.py:298
  13.9 0.0 copy-done.1
  13.9 0.0 copy-done.2
  13.9 0.0 copy-done
  13.9 0.0 copy-done.3
  13.9 6.7 %local_part.1 = (bf16[16,640,256]{2,1,0:T(8,128)(2,1)S(1)}, bf16[256,2048]{1,0:T(8,128)(2,1)S(1)}, bf16[256,2048]{1,0:T(8,128)(2,1)S(1)}, bf16[3,16,2048]{2,1,0:...) custom-call(bf16[3,256,2048]{2,1,0:T(8,128)(2,1)} %bitcast.17, bf16[256,2048]{1,0:T(8,128)(2,1)S(1)} %copy-done, ...), custom_call_target="tpu_custom_call" | custom-call | flops 1000000000 | bytes 16777216 | tf_op jit(solution)/shard_map/local_part/pallas_call | solution.py:164
  20.7 1.6 %collective-permute-done.2 = bf16[136,1152]{1,0:T(8,128)(2,1)S(1)} collective-permute-done((bf16[136,1152]{1,0:T(8,128)(2,1)S(1)}, bf16[136,1152]{1,0:T(8,128)(2,1)S(1)}, u32[]{:S(2)}, u32[]{:S(2)}) %collective-permute-start.2) | collective-permute-done | bytes 313376 | tf_op jit(solution)/shard_map/ppermute | solution.py:298
  22.2 0.0 collective-permute-done.3
  22.2 0.1 add.3.carry_ref
  22.3 1.1 %head_part.3 = (bf16[160,1152]{1,0:T(8,128)(2,1)S(1)}, f32[256,128]{1,0:T(8,128)S(1)}) custom-call(bf16[136,1152]{1,0:T(8,128)(2,1)S(1)} %add.3.carry_ref, bf16[3,16,2048]{2,1,0:T(8,128)(2,1)S(1)} %get-tuple-element.17.first_ref, bf16[256,2048]{1,0:T(8,128)(2,1)S(1)} %copy-done, f32[3,3,2048]{2,1,0:T(4,128)S(1)} %copy-done.1, f32[1,2048]{1,0:T(1,128)S(1)} %bitcast.9, ...), custom_call_target="tpu_custom_call" | custom-call | tf_op jit(solution)/shard_map/head_part/pallas_call | solution.py:229
  23.4 2.5 %collective-permute-done.1.carry_ref = bf16[136,640]{1,0:T(8,128)(2,1)S(1)} collective-permute-done((bf16[136,640]{1,0:T(8,128)(2,1)S(1)}, bf16[136,640]{1,0:T(8,128)(2,1)S(1)}, u32[]{:S(2)}, u32[]{:S(2)}) %collective-permute-start.1) | collective-permute-done | bytes 174112 | tf_op jit(solution)/shard_map/ppermute | solution.py:298
  25.9 0.7 %head_part.4 = (bf16[160,640]{1,0:T(8,128)(2,1)S(1)}, f32[256,128]{1,0:T(8,128)S(1)}) custom-call(bf16[136,640]{1,0:T(8,128)(2,1)S(1)} %collective-permute-done.1.carry_ref, bf16[3,16,2048]{2,1,0:T(8,128)(2,1)S(1)} %get-tuple-element.17.first_ref, bf16[256,2048]{1,0:T(8,128)(2,1)S(1)} %copy-done, f32[3,3,2048]{2,1,0:T(4,128)S(1)} %copy-done.1, ...), custom_call_target="tpu_custom_call" | custom-call | tf_op jit(solution)/shard_map/head_part/pallas_call | solution.py:229
  26.6 0.0 copy-start.4
  26.7 0.8 %collective-permute-done.carry_ref = bf16[136,256]{1,0:T(8,128)(2,1)S(1)} collective-permute-done((bf16[136,256]{1,0:T(8,128)(2,1)S(1)}, bf16[136,256]{1,0:T(8,128)(2,1)S(1)}, u32[]{:S(2)}, u32[]{:S(2)}) %collective-permute-start) | collective-permute-done | bytes 69664 | tf_op jit(solution)/shard_map/ppermute | solution.py:298
  27.4 0.5 %head_part.5 = (bf16[160,256]{1,0:T(8,128)(2,1)S(1)}, f32[8,256]{1,0:T(8,128)S(1)}) custom-call(bf16[136,256]{1,0:T(8,128)(2,1)S(1)} %collective-permute-done.carry_ref, bf16[3,16,2048]{2,1,0:T(8,128)(2,1)S(1)} %get-tuple-element.17.first_ref, bf16[256,2048]{1,0:T(8,128)(2,1)S(1)} %copy-done, f32[3,3,2048]{2,1,0:T(4,128)S(1)} %copy-done.1, ...), custom_call_target="tpu_custom_call" | custom-call | tf_op jit(solution)/shard_map/head_part/pallas_call | solution.py:229
  27.9 6.1 %all-gather = f32[4,1,256]{2,1,0:T(1,128)S(1)} all-gather(f32[1,1,256]{2,1,0:T(1,128)S(1)} %slice_bitcast_fusion), channel_id=1, replica_groups=mesh['ctx'=128,'tp'=4] {'tp'}, dimensions={0}, use_global_device_ids=true | all-gather | bytes 5120 | tf_op jit(solution)/shard_map/all_gather | solution.py:306
  34.1 0.0 copy-done.4
  34.1 1.2 %normalize.1 = bf16[256,2048]{1,0:T(8,128)(2,1)} custom-call(f32[4,256]{1,0:T(4,128)S(1)} %bitcast.12, bf16[160,1152]{1,0:T(8,128)(2,1)S(1)} %get-tuple-element.25.refs_0_, bf16[160,640]{1,0:T(8,128)(2,1)S(1)} %get-tuple-element.26.refs_1_, bf16[160,256]{1,0:T(8,128)(2,1)S(1)} %get-tuple-element.27.refs_2_, bf16[96,2048]{1,0:T(8,128)(2,1)S(1)} %get-tuple-element.28.refs_3_, ...), custom_call_target="tpu_custom_call" | custom-call | tf_op jit(solution)/shard_map/normalize/pallas_call | solution.py:276
  (2 shorter events, 0.0 us)
Async XLA Ops:
  0.0 13.9 %copy-start.1 = (f32[3,3,2048]{2,1,0:T(4,128)S(1)}, f32[3,3,2048]{2,1,0:T(4,128)}, u32[]{:S(2)}) copy-start(f32[3,3,2048]{2,1,0:T(4,128)} %short_ref.13) | copy-start | bytes 221188
  0.0 13.9 %copy-start.2 = (f32[2048]{0:T(1024)S(1)}, f32[2048]{0:T(1024)}, u32[]{:S(2)}) copy-start(f32[2048]{0:T(1024)} %param.10) | copy-start | bytes 24580
  0.0 13.9 %copy-start = (bf16[256,2048]{1,0:T(8,128)(2,1)S(1)}, bf16[256,2048]{1,0:T(8,128)(2,1)}, u32[]{:S(2)}) copy-start(bf16[256,2048]{1,0:T(8,128)(2,1)} %res_ref.7) | copy-start | bytes 3145732
  0.0 13.9 %copy-start.3 = (bf16[128,128]{1,0:T(8,128)(2,1)S(1)}, bf16[128,128]{1,0:T(8,128)(2,1)}, u32[]{:S(2)}) copy-start(bf16[128,128]{1,0:T(8,128)(2,1)} %filt_ref.1) | copy-start | bytes 98308
  1.7 20.5 %collective-permute-start.2 = (bf16[136,1152]{1,0:T(8,128)(2,1)S(1)}, bf16[136,1152]{1,0:T(8,128)(2,1)S(1)}, u32[]{:S(2)}, u32[]{:S(2)}) collective-permute-start(bf16[136,1152]{1,0:T(8,128)(2,1)S(1)} %tail_gate.5), channel_id=1, source_target_pairs={{0,4},{4,8},{8,12},{12,16},{16,20},{20,24},{24,28},{28,32},{32,36}... | collective-permute-start | bytes 940040 | tf_op jit(solution)/shard_map/ppermute | solution.py:298
  4.9 17.4 %collective-permute-start.3 = (bf16[136,1152]{1,0:T(8,128)(2,1)S(1)}, bf16[136,1152]{1,0:T(8,128)(2,1)S(1)}, u32[]{:S(2)}, u32[]{:S(2)}) collective-permute-start(bf16[136,1152]{1,0:T(8,128)(2,1)S(1)} %tail_gate.5), channel_id=1, source_target_pairs={{248,252},{249,253},{250,254},{251,255}} | collective-permute-start | bytes 940040 | tf_op jit(solution)/shard_map/ppermute | solution.py:299
  6.9 19.1 %collective-permute-start.1 = (bf16[136,640]{1,0:T(8,128)(2,1)S(1)}, bf16[136,640]{1,0:T(8,128)(2,1)S(1)}, u32[]{:S(2)}, u32[]{:S(2)}) collective-permute-start(bf16[136,640]{1,0:T(8,128)(2,1)S(1)} %tail_gate.4), channel_id=1, source_target_pairs={{0,4},{4,8},{8,12},{12,16},{16,20},{20,24},{24,28},{28,32},{32,36}... | collective-permute-start | bytes 522248 | tf_op jit(solution)/shard_map/ppermute | solution.py:298
  11.1 16.4 %collective-permute-start = (bf16[136,256]{1,0:T(8,128)(2,1)S(1)}, bf16[136,256]{1,0:T(8,128)(2,1)S(1)}, u32[]{:S(2)}, u32[]{:S(2)}) collective-permute-start(bf16[136,256]{1,0:T(8,128)(2,1)S(1)} %tail_gate.3), channel_id=1, source_target_pairs={{0,4},{4,8},{8,12},{12,16},{16,20},{20,24},{24,28},{28,32},{32,36}... | collective-permute-start | bytes 208904 | tf_op jit(solution)/shard_map/ppermute | solution.py:298
  26.6 7.4 %copy-start.4 = (f32[2048]{0:T(1024)S(1)}, f32[2048]{0:T(1024)}, u32[]{:S(2)}) copy-start(f32[2048]{0:T(1024)} %param.11) | copy-start | bytes 24580
